TPU v7x, 512 devices: a whole 4x4x16 slice. The times are simulated.
512 devices in a mesh: band: 128 (over z, y, x_lo), domain: 4 (over x_hi, core).
Axes of the slice: x: 4 (x_hi: 2, x_lo: 2; x = x_hi * 2 + x_lo), y: 4, z: 16, core: 2. Of those that a mesh axis runs over, the one named last changes fastest.
Arguments:
- orbitals: bfloat16 [1024, 8, 5120], P('band', 'domain'), may hold values from -6 to 6
- boundary: bfloat16 [1024, 4, 5120], P('band'), may hold values from -6 to 6
- potential: bfloat16 [8, 5120], P('domain'), may hold values from 0 to 2
Outputs:
- correlation: float32 [1024, 1024], P('band', 'domain')
- projected: float32 [1024, 1024], P('band', 'domain')
All inputs are finite; a program needn't handle non-finite values.
Results may differ from a plain program's by a relative error of at most 0.0012.
Values may be sent and summed in bfloat16 or wider, within the bound.
No kernel may reach another device: no remote copies, remote signals or barrier semaphores. Data moves between devices by JAX's collectives and lax.ppermute only.
A program may use at most 128 MiB of HBM per device.

v0:
```python
import jax
import jax.numpy as jnp
from jax import lax
from jax.sharding import PartitionSpec as P

NX = 160
NY = 32
NZ_DEV = 2
DEGREE = 4


filter_center = 5.5
filter_radius = 4.5


def padded_2(cells, sides, width):
    for axis, dim in sides:
        count = lax.axis_size(axis)
        ends = count - 1
        head = lax.slice_in_dim(cells, 0, width, axis=dim)
        tail = lax.slice_in_dim(cells, cells.shape[dim] - width, cells.shape[dim], axis=dim)
        cells = jnp.concatenate(
            [
                lax.ppermute(tail, axis, [(i, (i + 1) % count) for i in range(ends)]),
                cells,
                lax.ppermute(head, axis, [((i + 1) % count, i) for i in range(ends)]),
            ],
            axis=dim,
        )
    return cells


def second_diff(values, axis_pos):
    near = jnp.roll(values, 1, axis_pos) + jnp.roll(values, -1, axis_pos)
    far = jnp.roll(values, 2, axis_pos) + jnp.roll(values, -2, axis_pos)
    return (16.0 * near - far - 30.0 * values) / 12.0


def plane_part(values):
    shaped = values.reshape(values.shape[:-1] + (NY, NX))
    total = second_diff(shaped, -1) + second_diff(shaped, -2)
    return total.reshape(values.shape)


def hamiltonian(padded, potential):
    middle = padded[:, 2:-2]
    z_part = (
        16.0 * (padded[:, 1:-3] + padded[:, 3:-1])
        - (padded[:, :-4] + padded[:, 4:])
        - 30.0 * middle
    ) / 12.0
    laplace = z_part + plane_part(middle)
    return -0.5 * laplace + potential.astype(jnp.float32) * middle


def chebyshev(apply_ham, orb_block):
    earlier = orb_block
    current = (
        (apply_ham(orb_block) - filter_center * orb_block.astype(jnp.float32)) / filter_radius
    ).astype(jnp.bfloat16)
    for degree_step in range(DEGREE - 1):
        following = (
            2.0 * (apply_ham(current) - filter_center * current.astype(jnp.float32)) / filter_radius
        )
        following = (following - earlier.astype(jnp.float32)).astype(jnp.bfloat16)
        earlier, current = (current, following)
    return (current, apply_ham(current).astype(jnp.bfloat16))


def per_device(orbitals, boundary, potential):
    orb_count = orbitals.shape[0]
    domain_pos = lax.axis_index("domain")
    domain_count = lax.axis_size("domain")
    last_pos = domain_count - 1

    def apply_ham(values):
        padded = padded_2(values, (("domain", 1),), 2)
        lower_rim = jnp.where(domain_pos == 0, boundary[:, 0:2], padded[:, 0:2])
        upper_rim = jnp.where(domain_pos == last_pos, boundary[:, 2:4], padded[:, -2:])
        padded = jnp.concatenate([lower_rim, padded[:, 2:-2], upper_rim], axis=1).astype(
            jnp.float32
        )
        return hamiltonian(padded, potential)

    filtered, applied = chebyshev(apply_ham, orbitals)
    filtered = filtered.reshape(orb_count, -1)
    applied = applied.reshape(orb_count, -1)
    cell_y, cell_h = (
        lax.all_to_all(filtered, "band", split_axis=1, concat_axis=0, tiled=True),
        lax.all_to_all(applied, "band", split_axis=1, concat_axis=0, tiled=True),
    )
    cell_y, cell_h = (
        lax.all_gather(cell_y, "domain", axis=1, tiled=True),
        lax.all_gather(cell_h, "domain", axis=1, tiled=True),
    )
    column_count = cell_y.shape[0] // domain_count
    column_y = lax.dynamic_slice_in_dim(cell_y, domain_pos * column_count, column_count, 0)
    column_h = lax.dynamic_slice_in_dim(cell_h, domain_pos * column_count, column_count, 0)
    contract_dims = (((1,), (1,)), ((), ()))
    with_y = lax.dot_general(cell_y, column_y, contract_dims, preferred_element_type=jnp.float32)
    with_h = lax.dot_general(cell_y, column_h, contract_dims, preferred_element_type=jnp.float32)
    summed = lax.psum_scatter(
        jnp.concatenate([with_y, with_h], axis=1), "band", scatter_dimension=0, tiled=True
    )
    total_cells = NZ_DEV * NY * NX * domain_count
    correlation = summed[:, :column_count] / total_cells
    projected = summed[:, column_count:] / total_cells
    return (correlation, projected)


def solution(mesh):
    return jax.shard_map(
        per_device,
        mesh=mesh,
        in_specs=(P("band", "domain", None), P("band", None, None), P("domain", None)),
        out_specs=(P("band", "domain"), P("band", "domain")),
        check_vma=False,
    )
```

profile of v0, /device:TPU:6, one launch (start us, length us, event | category | flops | bytes accessed | tf_op | source)
XLA Modules:
  0.0 792.8 jit_solution(4684403561107533573)
XLA Ops:
  7.2 0.9 copy.20
  8.1 2.8 collective-permute-start.1
  10.9 1.9 collective-permute-start
  12.8 1.4 fusion.109
  15.0 4.0 collective-permute-done
  20.0 0.9 fusion.104
  20.8 1.0 fusion.101
  23.0 1.0 sub.167
  24.0 1.8 fusion.1
  26.1 1.2 fusion.22
  27.3 1.9 collective-permute-start.3
  29.2 2.4 collective-permute-start.2
  32.1 5.3 collective-permute-done.2
  38.3 0.9 fusion.96
  39.2 1.1 fusion.93
  40.3 0.9 fusion.94
  41.5 1.0 sub.176
  42.5 2.0 fusion.5
  44.8 1.2 fusion.23
  46.0 1.9 collective-permute-start.5
  47.9 2.4 collective-permute-start.4
  50.8 5.3 collective-permute-done.4
  57.0 0.9 fusion.88
  57.9 1.1 fusion.85
  60.2 1.0 sub.186
  61.2 2.0 fusion.9
  63.5 1.2 fusion.26
  64.7 1.9 collective-permute-start.7
  66.6 2.6 collective-permute-start.6
  69.5 5.3 collective-permute-done.6
  75.7 0.9 fusion.80
  76.6 1.1 fusion.77
  78.9 1.0 sub.196
  79.9 2.0 fusion.13
  82.2 1.2 fusion.29
  83.4 1.9 collective-permute-start.9
  85.5 2.4 collective-permute-start.8
  89.1 21.0 %all-to-all-start = ((bf16[8,128,80]{2,0,1:T(8,128)(2,1)}), bf16[8,128,80]{2,0,1:T(8,128)(2,1)}, u32[]{:S(2)}, u32[]{:S(2)}) async-start(bf16[8,128,80]{2,0,1:T(8,128)(2,1)} %copy.26), calls=%async_computation | async-start | bytes 524288 | tf_op jit(solution)/shard_map/all_to_all | solution.py:89
  111.9 1.0 fusion.69
  114.3 1.8 fusion.17
  117.9 11.4 %all-to-all-done = bf16[8,128,80]{2,0,1:T(8,128)(2,1)} async-done(((bf16[8,128,80]{2,0,1:T(8,128)(2,1)}), bf16[8,128,80]{2,0,1:T(8,128)(2,1)}, u32[]{:S(2)}, u32[]{:S(2)}) %all-to-all-start) | async-done | bytes 163872 | tf_op jit(solution)/shard_map/all_to_all | solution.py:89
  129.3 8.8 %all-to-all-start.1 = ((bf16[8,128,80]{2,0,1:T(8,128)(2,1)}), bf16[8,128,80]{2,0,1:T(8,128)(2,1)S(1)}, u32[]{:S(2)}, u32[]{:S(2)}) async-start(bf16[8,128,80]{2,0,1:T(8,128)(2,1)} %copy.29), calls=%async_computation.1 | async-start | bytes 524288 | tf_op jit(solution)/shard_map/all_to_all | solution.py:90
  138.2 1.1 copy.27
  139.3 9.0 %all_gather.6 = bf16[1024,320]{0,1:T(8,128)(2,1)S(1)} all-gather(bf16[1024,80]{0,1:T(8,128)(2,1)S(1)} %copy.27), channel_id=1, replica_groups=mesh['band'=128,'domain'=4] {'domain'}, dimensions={1}, use_global_device_ids=true | all-gather | bytes 819200 | tf_op jit(solution)/shard_map/all_gather | solution.py:93
  148.8 8.4 %all-to-all-done.1 = bf16[8,128,80]{2,0,1:T(8,128)(2,1)S(1)} async-done(((bf16[8,128,80]{2,0,1:T(8,128)(2,1)}), bf16[8,128,80]{2,0,1:T(8,128)(2,1)S(1)}, u32[]{:S(2)}, u32[]{:S(2)}) %all-to-all-start.1) | async-done | bytes 163872 | tf_op jit(solution)/shard_map/all_to_all | solution.py:90
  157.3 8.4 %all_gather.7 = bf16[1024,320]{0,1:T(8,128)(2,1)S(1)} all-gather(bf16[1024,80]{0,1:T(8,128)(2,1)S(1)} %copy.30), channel_id=1, replica_groups=mesh['band'=128,'domain'=4] {'domain'}, dimensions={1}, use_global_device_ids=true | all-gather | bytes 819200 | tf_op jit(solution)/shard_map/all_gather | solution.py:94
  166.3 1.8 copy.33
  168.2 615.4 %reduce-scatter.4.cloned.1.call-done = f32[8,512]{1,0:T(8,128)} async-done(((f32[1024,512]{1,0:T(8,128)}), f32[8,512]{1,0:T(8,128)}) %reduce-scatter.4.cloned.1.call-update) | async-done | bytes 16400
  (95 shorter events, 20.2 us)
Async XLA Ops:
  8.1 6.8 collective-permute-start.1
  10.9 8.1 %collective-permute-start = (bf16[8,2,5120]{2,0,1:T(8,128)(2,1)S(1)}, bf16[8,2,5120]{2,0,1:T(8,128)(2,1)S(1)}, u32[]{:S(2)}, u32[]{:S(2)}) collective-permute-start(bf16[8,2,5120]{2,0,1:T(8,128)(2,1)S(1)} %copy.20), channel_id=1, source_target_pairs={{0,1},{1,2},{2,3},{4,5},{5,6},{6,7},{8,9},{9,10},{10,11},{12,13},{... | collective-permute-start | bytes 491528 | tf_op jit(solution)/shard_map/ppermute | solution.py:24
  27.3 4.7 collective-permute-start.3
  29.2 8.1 %collective-permute-start.2 = (bf16[8,2,5120]{2,0,1:T(8,128)(2,1)S(1)}, bf16[8,2,5120]{2,0,1:T(8,128)(2,1)S(1)}, u32[]{:S(2)}, u32[]{:S(2)}) collective-permute-start(bf16[8,2,5120]{2,0,1:T(8,128)(2,1)S(1)} %fusion.22), channel_id=1, source_target_pairs={{0,1},{1,2},{2,3},{4,5},{5,6},{6,7},{8,9},{9,10},{10,11},{12,13},{... | collective-permute-start | bytes 491528 | tf_op jit(solution)/shard_map/ppermute | solution.py:24
  42.5 2.3 copy-start
  46.0 4.7 collective-permute-start.5
  47.9 8.1 %collective-permute-start.4 = (bf16[8,2,5120]{2,0,1:T(8,128)(2,1)S(1)}, bf16[8,2,5120]{2,0,1:T(8,128)(2,1)S(1)}, u32[]{:S(2)}, u32[]{:S(2)}) collective-permute-start(bf16[8,2,5120]{2,0,1:T(8,128)(2,1)S(1)} %fusion.23), channel_id=1, source_target_pairs={{0,1},{1,2},{2,3},{4,5},{5,6},{6,7},{8,9},{9,10},{10,11},{12,13},{... | collective-permute-start | bytes 491528 | tf_op jit(solution)/shard_map/ppermute | solution.py:24
  64.7 4.7 collective-permute-start.7
  66.6 8.1 %collective-permute-start.6 = (bf16[8,2,5120]{2,0,1:T(8,128)(2,1)S(1)}, bf16[8,2,5120]{2,0,1:T(8,128)(2,1)S(1)}, u32[]{:S(2)}, u32[]{:S(2)}) collective-permute-start(bf16[8,2,5120]{2,0,1:T(8,128)(2,1)S(1)} %fusion.26), channel_id=1, source_target_pairs={{0,1},{1,2},{2,3},{4,5},{5,6},{6,7},{8,9},{9,10},{10,11},{12,13},{... | collective-permute-start | bytes 491528 | tf_op jit(solution)/shard_map/ppermute | solution.py:24
  83.4 26.7 %collective-permute-start.9 = (bf16[8,2,5120]{2,0,1:T(8,128)(2,1)S(1)}, bf16[8,2,5120]{2,0,1:T(8,128)(2,1)S(1)}, u32[]{:S(2)}, u32[]{:S(2)}) collective-permute-start(bf16[8,2,5120]{2,0,1:T(8,128)(2,1)S(1)} %fusion.29), channel_id=1, source_target_pairs={{1,0},{2,1},{3,2},{5,4},{6,5},{7,6},{9,8},{10,9},{11,10},{13,12},{... | collective-permute-start | bytes 491528 | tf_op jit(solution)/shard_map/ppermute | solution.py:26
  85.5 24.6 %collective-permute-start.8 = (bf16[8,2,5120]{2,0,1:T(8,128)(2,1)S(1)}, bf16[8,2,5120]{2,0,1:T(8,128)(2,1)S(1)}, u32[]{:S(2)}, u32[]{:S(2)}) collective-permute-start(bf16[8,2,5120]{2,0,1:T(8,128)(2,1)S(1)} %fusion.29), channel_id=1, source_target_pairs={{0,1},{1,2},{2,3},{4,5},{5,6},{6,7},{8,9},{9,10},{10,11},{12,13},{... | collective-permute-start | bytes 491528 | tf_op jit(solution)/shard_map/ppermute | solution.py:24
  89.1 40.3 %all-to-all-start = ((bf16[8,128,80]{2,0,1:T(8,128)(2,1)}), bf16[8,128,80]{2,0,1:T(8,128)(2,1)}, u32[]{:S(2)}, u32[]{:S(2)}) async-start(bf16[8,128,80]{2,0,1:T(8,128)(2,1)} %copy.26), calls=%async_computation | async-start | bytes 524288 | tf_op jit(solution)/shard_map/all_to_all | solution.py:89
  129.3 27.8 %all-to-all-start.1 = ((bf16[8,128,80]{2,0,1:T(8,128)(2,1)}), bf16[8,128,80]{2,0,1:T(8,128)(2,1)S(1)}, u32[]{:S(2)}, u32[]{:S(2)}) async-start(bf16[8,128,80]{2,0,1:T(8,128)(2,1)} %copy.29), calls=%async_computation.1 | async-start | bytes 524288 | tf_op jit(solution)/shard_map/all_to_all | solution.py:90
  138.1 645.5 %reduce-scatter.4.cloned.1.call-start = ((), (), s32[]{:S(2)}) async-start(), calls=%async_computation.3 | async-start | bytes 2113536
Sparse Core Ops, SparseCore 0:
  168.3 615.2 reduce-scatter.3
where the time goes:
time: 798 us; the launch traced here: 793 us
  waiting for transfers between devices  656 us (82%)
  starting transfers between devices  52 us (7%)
  local copies, waits for them, and re-layouts  33.8 us (4%)
  other arithmetic  17.8 us (2%)
  blocking collectives  17.4 us (2%)
  between operations  14.7 us (2%)
    unnamed x2, waiting for transfers between devices  615 us
    all_to_all x1, starting transfers between devices, per_device(): lax.all_to_all(filtered, 'band', split_axis=1, concat_axis=0, tiled=True)  21 us
    ppermute x5, waiting for transfers between devices, padded_2(): lax.ppermute(tail, axis, [(i, (i + 1) % count) for i in range(ends)])  19.9 us
  transfers between devices with their start and end apart: 13, of which 10 were waited for; matrix products, arithmetic and copies ran while one was open for 2% of the time, Pallas kernels for 0%

commit v1 on v0

v1 whole, which is shorter than its diff:
```python
import functools
import jax
import jax.numpy as jnp
from jax import lax
from jax.experimental import pallas as pl
from jax.experimental.pallas import tpu as pltpu
from jax.sharding import Mesh, PartitionSpec as P

NX = 160
NY = 32
NZ = 8
PLANE = NX * NY
DEGREE = 4
ORBS = 8
PAD = 384
SPAN = 640
CHUNKS = PLANE // SPAN
SHARES = 32
SHARE = NZ * PLANE // SHARES

filter_center = 5.5
filter_radius = 4.5


def filter_kernel(which, mixed_ref, rim_ref, out_ref, one, two, rim_term, pot):
    del which
    row = lax.broadcasted_iota(jnp.int32, (NZ, SPAN), 0)
    x = lax.rem(lax.broadcasted_iota(jnp.int32, (NZ, SPAN), 1), NX)
    zero = jnp.zeros((NZ, SPAN), jnp.float32)
    below_1 = jnp.where(row >= 1, zero + 16.0, zero)
    above_1 = jnp.where(row <= NZ - 2, zero + 16.0, zero)
    below_2 = jnp.where(row >= 2, zero + 1.0, zero)
    above_2 = jnp.where(row <= NZ - 3, zero + 1.0, zero)
    first, last = x == 0, x == NX - 1
    first_two, last_two = x <= 1, x >= NX - 2

    def wrap(ref, orb):
        ref[orb, :, 0:PAD] = ref[orb, :, PLANE : PLANE + PAD]
        ref[orb, :, PAD + PLANE : 2 * PAD + PLANE] = ref[orb, :, PAD : 2 * PAD]

    pot[...] = jnp.concatenate([mixed_ref[s, 4:6, :] for s in range(4)], axis=0).astype(jnp.float32)
    for orb in range(2):
        planes = [mixed_ref[s, 2 * orb : 2 * orb + 2, :] for s in range(4)]
        one[orb, :, PAD : PAD + PLANE] = jnp.concatenate(planes, axis=0).astype(jnp.float32)
        wrap(one, orb)
        rim = rim_ref[0, orb].astype(jnp.float32)
        low_far, low, high, high_far = (rim[k : k + 1] for k in range(4))
        rim_term[orb] = jnp.concatenate(
            [16.0 * low - low_far, -low, jnp.zeros((4, PLANE), jnp.float32), -high, 16.0 * high - high_far],
            axis=0,
        )

    def apply_ham(ref, orb, at):
        window = ref[orb, :, pl.ds(at, SPAN + 2 * PAD)]
        width = SPAN + 2 * PAD

        def cells(shift):
            return pltpu.roll(window, (-shift) % width, 1)[:, PAD : PAD + SPAN]

        middle = window[:, PAD : PAD + SPAN]
        near = jnp.where(first, cells(NX - 1), cells(-1)) + jnp.where(last, cells(1 - NX), cells(1))
        near = near + (cells(NX) + cells(-NX))
        far = jnp.where(first_two, cells(NX - 2), cells(-2)) + jnp.where(
            last_two, cells(2 - NX), cells(2)
        )
        far = far + (cells(2 * NX) + cells(-2 * NX))
        z_near = below_1 * pltpu.roll(middle, 1, 0) + above_1 * pltpu.roll(middle, NZ - 1, 0)
        z_far = below_2 * pltpu.roll(middle, 2, 0) + above_2 * pltpu.roll(middle, NZ - 2, 0)
        total = (16.0 * near - far) + (z_near - z_far) - 90.0 * middle
        total = total + rim_term[orb, :, pl.ds(at, SPAN)]
        return total * (-0.5 / 12.0) + pot[:, pl.ds(at, SPAN)] * middle, middle

    current, earlier = one, two
    for step in range(DEGREE):

        def body(chunk, carry, step=step, current=current, earlier=earlier):
            at = pl.multiple_of(chunk * SPAN, SPAN)
            for orb in range(2):
                with_h, middle = apply_ham(current, orb, at)
                following = (with_h - filter_center * middle) * (1.0 / filter_radius)
                place = (orb, slice(None), pl.ds(at + PAD, SPAN))
                if step > 0:
                    following = 2.0 * following - earlier[place]
                earlier[place] = following.astype(jnp.bfloat16).astype(jnp.float32)
            return carry

        lax.fori_loop(0, CHUNKS, body, 0)
        for orb in range(2):
            wrap(earlier, orb)
        current, earlier = earlier, current

    def last_body(chunk, carry):
        at = pl.multiple_of(chunk * SPAN, SPAN)
        for orb in range(2):
            with_h, middle = apply_ham(current, orb, at)
            out_ref[orb, :, pl.ds(at, SPAN)] = middle.astype(jnp.bfloat16)
            out_ref[2 + orb, :, pl.ds(at, SPAN)] = with_h.astype(jnp.bfloat16)
        return carry

    lax.fori_loop(0, CHUNKS, last_body, 0)


def filtered_and_applied(which, mixed, boundary):
    return pl.pallas_call(
        filter_kernel,
        grid_spec=pltpu.PrefetchScalarGridSpec(
            num_scalar_prefetch=1,
            grid=(1,),
            in_specs=[
                pl.BlockSpec((4, 6, PLANE), lambda i, which: (0, 0, 0)),
                pl.BlockSpec((1, 2, 4, PLANE), lambda i, which: (which[0], 0, 0, 0)),
            ],
            out_specs=pl.BlockSpec((4, NZ, PLANE), lambda i, which: (0, 0, 0)),
            scratch_shapes=[
                pltpu.VMEM((2, NZ, PLANE + 2 * PAD), jnp.float32),
                pltpu.VMEM((2, NZ, PLANE + 2 * PAD), jnp.float32),
                pltpu.VMEM((2, NZ, PLANE), jnp.float32),
                pltpu.VMEM((NZ, PLANE), jnp.float32),
            ],
        ),
        out_shape=jax.ShapeDtypeStruct((4, NZ, PLANE), jnp.bfloat16),
        compiler_params=pltpu.CompilerParams(vmem_limit_bytes=24 * 1024 * 1024),
        name="chebyshev_filter",
    )(which, mixed, boundary)


def per_device(orbitals, boundary, potential, trade):
    own = lax.axis_index("d")
    pieces = orbitals.reshape(4, 4, PLANE)
    pieces = jnp.concatenate([pieces, jnp.broadcast_to(potential[None], (4, 2, PLANE))], axis=1)
    mixed = lax.all_to_all(pieces, "d", split_axis=0, concat_axis=0, tiled=True)
    fields = filtered_and_applied(
        own.astype(jnp.int32).reshape(1), mixed, boundary.reshape(4, 2, 4, PLANE)
    )
    shares = fields.reshape(4, SHARES, SHARE).transpose(1, 0, 2)
    shares = lax.all_to_all(shares, ("y", "xl", "d"), split_axis=0, concat_axis=0, tiled=True)
    shares = shares.reshape(SHARES, 2, 2, SHARE).transpose(1, 0, 2, 3).reshape(2, 64, SHARE)
    columns = lax.all_gather(shares, "zl", axis=1, tiled=True).reshape(512, SHARE)
    rows = lax.all_gather(shares[0], "zh", axis=0, tiled=True)
    partial = lax.dot_general(
        rows, columns, (((1,), (1,)), ((), ())), preferred_element_type=jnp.float32
    )
    partial = partial.reshape(4, 8, ORBS, 512).transpose(1, 0, 2, 3).reshape(SHARES, ORBS, 512)
    parts = lax.all_to_all(partial, ("y", "xl", "d"), split_axis=0, concat_axis=0, tiled=True)
    summed = jnp.sum(parts, axis=0) * (1.0 / (NZ * PLANE))
    summed = lax.ppermute(summed, ("zh", "zl", "y", "xl", "d"), trade)
    return summed[:, :256], summed[:, 256:]


def solution(mesh):
    split = Mesh(mesh.devices.reshape(4, 4, 4, 2, 4), ("zh", "zl", "y", "xl", "d"))
    trade = []
    for zh in range(4):
        for rest in range(32):
            for d in range(4):
                trade.append(((zh * 32 + rest) * 4 + d, (d * 32 + rest) * 4 + zh))
    band = ("zh", "zl", "y", "xl")
    return jax.shard_map(
        functools.partial(per_device, trade=trade),
        mesh=split,
        in_specs=(P(band, "d", None), P(band, None, None), P("d", None)),
        out_specs=(P(band, "d"), P(band, "d")),
        check_vma=False,
    )
```

time: 798 us -> 146 us (0.18)
  waiting for transfers between devices: 656 us -> 30.5 us
  blocking collectives: 17.4 us -> 70.7 us
  starting transfers between devices: 52 us -> 13.3 us
  local copies, waits for them, and re-layouts: 33.8 us -> 4.29 us
  other arithmetic: 17.8 us -> 0.94 us
  Pallas kernels: 0 us -> 9.85 us
    unnamed x2 -> x1, waiting for transfers between devices: 615 us -> 0.02 us
    all_to_all x0 -> x2, blocking collectives: none -> 33.6 us  [the longest x1 18.4 us: per_device(): lax.all_to_all(shares, ('y', 'xl', 'd'), split_axis=0, concat_axis=0, til...]
    all_to_all x2 -> x1, starting transfers between devices: 29.8 us -> 4.83 us  [per_device(): mixed = lax.all_to_all(pieces, 'd', split_axis=0, concat_axis=0, tiled=True)]
    all_gather x2 -> x1, blocking collectives: 17.4 us -> 37.1 us  [per_device(): rows = lax.all_gather(shares[0], 'zh', axis=0, tiled=True)]
    slice x47 -> x2, local copies, waits for them, and re-layouts: 18.6 us -> 0.72 us  [the longest x1 0.6 us: per_device(): return (summed[:, :256], summed[:, 256:])]
    all_gather x0 -> x1, waiting for transfers between devices: none -> 17.2 us  [per_device(): lax.all_gather(shares, 'zl', axis=1, tiled=True).reshape(512, SHARE)]
    all_to_all x2 -> x1, waiting for transfers between devices: 19.8 us -> 5.07 us  [per_device(): mixed = lax.all_to_all(pieces, 'd', split_axis=0, concat_axis=0, tiled=True)]
    ppermute x10 -> x1, starting transfers between devices: 22.2 us -> 8.49 us  [per_device(): summed = lax.ppermute(summed, ('zh', 'zl', 'y', 'xl', 'd'), trade)]
  transfers between devices with their start and end apart: 13 -> 3, of which waited for: 10 -> 3; matrix products, arithmetic and copies ran while one was open for 2% -> 0% of each run, Pallas kernels for 0% -> 0%
where the time goes in v1:
time: 146 us
  blocking collectives  70.7 us (48%)
  waiting for transfers between devices  30.5 us (21%)
  between operations  14.1 us (10%)
  starting transfers between devices  13.3 us (9%)
  Pallas kernels  9.85 us (7%)
  local copies, waits for them, and re-layouts  4.29 us (3%)
  matrix products  1.86 us (1%)
    all_gather x1, blocking collectives, per_device(): rows = lax.all_gather(shares[0], 'zh', axis=0, tiled=True)  37.1 us
    all_to_all x1, blocking collectives, per_device(): lax.all_to_all(shares, ('y', 'xl', 'd'), split_axis=0, concat_axis=0, til...  18.4 us
    all_gather x1, waiting for transfers between devices, per_device(): lax.all_gather(shares, 'zl', axis=1, tiled=True).reshape(512, SHARE)  17.2 us
    all_to_all x1, blocking collectives, per_device(): lax.all_to_all(partial, ('y', 'xl', 'd'), split_axis=0, concat_axis=0, ti...  15.1 us
    pallas_call x1, Pallas kernels, filtered_and_applied(): pl.pallas_call(filter_kernel, grid_spec=pltpu.PrefetchScalarGridSpec(num_...  9.85 us
    ppermute x1, starting transfers between devices, per_device(): summed = lax.ppermute(summed, ('zh', 'zl', 'y', 'xl', 'd'), trade)  8.49 us
    ppermute x1, waiting for transfers between devices, per_device(): summed = lax.ppermute(summed, ('zh', 'zl', 'y', 'xl', 'd'), trade)  8.25 us
    all_to_all x1, waiting for transfers between devices, per_device(): mixed = lax.all_to_all(pieces, 'd', split_axis=0, concat_axis=0, tiled=True)  5.07 us
  transfers between devices with their start and end apart: 3, of which 3 were waited for; matrix products, arithmetic and copies ran while one was open for 0% of the time, Pallas kernels for 0%

profile of v1, /device:TPU:6, one launch (start us, length us, event | category | flops | bytes accessed | tf_op | source)
XLA Modules:
  0.0 145.6 jit_solution(16482537698125356797)
XLA Ops:
  7.2 0.0 copy-start
  7.2 1.0 reshape.34
  8.2 0.8 broadcast_in_dim.2
  9.0 0.9 pad_maximum_fusion
  9.9 4.8 %all-to-all-start = ((bf16[4,6,5120]{2,1,0:T(8,128)(2,1)}), bf16[4,6,5120]{2,1,0:T(8,128)(2,1)S(1)}, u32[]{:S(2)}, u32[]{:S(2)}) async-start(bf16[4,6,5120]{2,1,0:T(8,128)(2,1)} %pad_maximum_fusion), calls=%async_computation | async-start | bytes 655360 | tf_op jit(solution)/shard_map/all_to_all | solution.py:131
  14.7 0.0 all-gather.2.cloned.1.call-start
  14.7 5.1 %all-to-all-done.mixed_ref = bf16[4,6,5120]{2,1,0:T(8,128)(2,1)S(1)} async-done(((bf16[4,6,5120]{2,1,0:T(8,128)(2,1)}), bf16[4,6,5120]{2,1,0:T(8,128)(2,1)S(1)}, u32[]{:S(2)}, u32[]{:S(2)}) %all-to-all-start) | async-done | bytes 245792 | tf_op jit(solution)/shard_map/all_to_all | solution.py:131
  19.8 0.0 copy-done
  19.8 9.9 %chebyshev_filter.1 = bf16[4,8,5120]{2,1,0:T(8,128)(2,1)S(1)} custom-call(s32[1]{0:T(128)} %bitcast.which, bf16[4,6,5120]{2,1,0:T(8,128)(2,1)S(1)} %all-to-all-done.mixed_ref, bf16[4,2,4,5120]{3,2,1,0:T(4,128)(2,1)S(1)} %bitcast.19), custom_call_target="tpu_custom_call" | custom-call | tf_op jit(solution)/shard_map/chebyshev_filter/pallas_call | solution.py:104
  29.6 0.2 reshape.36
  29.8 0.3 copy.15
  30.1 18.4 %all_to_all.15 = bf16[32,4,1280]{2,1,0:T(4,128)(2,1)S(1)} all-to-all(bf16[32,4,1280]{2,1,0:T(4,128)(2,1)S(1)} %bitcast.25), channel_id=1, replica_groups=mesh['zh'=4,'zl'=4,'y'=4,'xl'=2,'d'=4] {'y','xl','d'}, dimensions={0} | all-to-all | bytes 655360 | tf_op jit(solution)/shard_map/all_to_all | solution.py:136
  48.5 0.1 reshape.37
  48.7 0.2 copy.11
  48.9 0.9 reshape.38
  49.7 0.0 all-gather.2.cloned.1.call-update
  49.8 0.1 slice.13
  49.9 0.1 squeeze.3
  50.0 37.1 %all_gather.6 = bf16[256,1280]{1,0:T(8,128)(2,1)S(1)} all-gather(bf16[64,1280]{1,0:T(8,128)(2,1)S(1)} %squeeze.3), channel_id=1, replica_groups=mesh['zh'=4,'zl'=4,'y'=4,'xl'=2,'d'=4] {'zh'}, dimensions={0}, use_global_device_ids=true | all-gather | bytes 819200 | tf_op jit(solution)/shard_map/all_gather | solution.py:139
  87.1 17.2 %all-gather.2.cloned.1.call-done = bf16[2,256,1280]{2,1,0:T(8,128)(2,1)} async-done(((bf16[2,64,1280]{2,1,0:T(8,128)(2,1)}), bf16[2,256,1280]{2,1,0:T(8,128)(2,1)}) %all-gather.2.cloned.1.call-update) | async-done | bytes 1310736 | tf_op jit(solution)/shard_map/all_gather | solution.py:138
  104.3 1.9 %convolution_bitcast_fusion = f32[8,4,8,512]{3,2,0,1:T(8,128)S(1)} fusion(bf16[4,8,8,1280]{3,2,1,0:T(8,128)(2,1)S(1)} %bitcast.20, bf16[512,1280,1,1]{1,0,3,2:T(8,128)(2,1)} %bitcast.24), kind=kOutput, calls=%fused_computation | convolution fusion | flops 335544320 | bytes 2490368 | tf_op jit(solution)/shard_map/dot_general | solution.py:140
  106.2 15.1 %all_to_all.16 = f32[32,8,512]{2,1,0:T(8,128)S(1)} all-to-all(f32[32,8,512]{2,1,0:T(8,128)S(1)} %bitcast.21), channel_id=1, replica_groups=mesh['zh'=4,'zl'=4,'y'=4,'xl'=2,'d'=4] {'y','xl','d'}, dimensions={0} | all-to-all | bytes 1048576 | tf_op jit(solution)/shard_map/all_to_all | solution.py:144
  121.4 8.5 %collective-permute-start = (f32[8,512]{1,0:T(8,128)S(1)}, f32[8,512]{1,0:T(8,128)S(1)}, u32[]{:S(2)}, u32[]{:S(2)}) collective-permute-start(f32[8,512]{1,0:T(8,128)S(1)} %broadcast_multiply_fusion), channel_id=1, source_target_pairs={{0,0},{1,128},{2,256},{3,384},{4,4},{5,132},{6,260},{7,388},{8,8},... | collective-permute-start | bytes 49160 | tf_op jit(solution)/shard_map/ppermute | solution.py:146
  129.9 8.3 %collective-permute-done = f32[8,512]{1,0:T(8,128)S(1)} collective-permute-done((f32[8,512]{1,0:T(8,128)S(1)}, f32[8,512]{1,0:T(8,128)S(1)}, u32[]{:S(2)}, u32[]{:S(2)}) %collective-permute-start) | collective-permute-done | bytes 16416 | tf_op jit(solution)/shard_map/ppermute | solution.py:146
  138.2 0.6 fusion
  (3 shorter events, 0.1 us)
Async XLA Ops:
  7.2 12.6 %copy-start = (bf16[8,4,5120]{2,1,0:T(4,128)(2,1)S(1)}, bf16[8,4,5120]{2,1,0:T(4,128)(2,1)}, u32[]{:S(2)}) copy-start(bf16[8,4,5120]{2,1,0:T(4,128)(2,1)} %param.4) | copy-start | bytes 983044
  9.9 9.9 %all-to-all-start = ((bf16[4,6,5120]{2,1,0:T(8,128)(2,1)}), bf16[4,6,5120]{2,1,0:T(8,128)(2,1)S(1)}, u32[]{:S(2)}, u32[]{:S(2)}) async-start(bf16[4,6,5120]{2,1,0:T(8,128)(2,1)} %pad_maximum_fusion), calls=%async_computation | async-start | bytes 655360 | tf_op jit(solution)/shard_map/all_to_all | solution.py:131
  14.7 89.6 %all-gather.2.cloned.1.call-start = ((), (), s32[]{:S(2)}) async-start(), calls=%async_computation.3 | async-start | bytes 1638400 | tf_op jit(solution)/shard_map/all_gather | solution.py:138
  121.4 16.7 %collective-permute-start = (f32[8,512]{1,0:T(8,128)S(1)}, f32[8,512]{1,0:T(8,128)S(1)}, u32[]{:S(2)}, u32[]{:S(2)}) collective-permute-start(f32[8,512]{1,0:T(8,128)S(1)} %broadcast_multiply_fusion), channel_id=1, source_target_pairs={{0,0},{1,128},{2,256},{3,384},{4,4},{5,132},{6,260},{7,388},{8,8},... | collective-permute-start | bytes 49160 | tf_op jit(solution)/shard_map/ppermute | solution.py:146
Sparse Core Ops, SparseCore 0:
  49.9 54.3 all-gather.1

commit v2 on v1

--- a/solution.py
+++ b/solution.py
@@ -1,4 +1,3 @@
-import functools
 import jax
 import jax.numpy as jnp
 from jax import lax
@@ -11,11 +10,10 @@
 NZ = 8
 PLANE = NX * NY
 DEGREE = 4
-ORBS = 8
 PAD = 384
 SPAN = 640
 CHUNKS = PLANE // SPAN
-SHARES = 32
+SHARES = 16
 SHARE = NZ * PLANE // SHARES
 
 filter_center = 5.5
@@ -74,7 +72,7 @@
     for step in range(DEGREE):
 
         def body(chunk, carry, step=step, current=current, earlier=earlier):
-            at = pl.multiple_of(chunk * SPAN, SPAN)
+            at = chunk * SPAN
             for orb in range(2):
                 with_h, middle = apply_ham(current, orb, at)
                 following = (with_h - filter_center * middle) * (1.0 / filter_radius)
@@ -84,20 +82,22 @@
                 earlier[place] = following.astype(jnp.bfloat16).astype(jnp.float32)
             return carry
 
-        lax.fori_loop(0, CHUNKS, body, 0)
+        for chunk in range(CHUNKS):
+            body(chunk, 0)
         for orb in range(2):
             wrap(earlier, orb)
         current, earlier = earlier, current
 
     def last_body(chunk, carry):
-        at = pl.multiple_of(chunk * SPAN, SPAN)
+        at = chunk * SPAN
         for orb in range(2):
             with_h, middle = apply_ham(current, orb, at)
             out_ref[orb, :, pl.ds(at, SPAN)] = middle.astype(jnp.bfloat16)
             out_ref[2 + orb, :, pl.ds(at, SPAN)] = with_h.astype(jnp.bfloat16)
         return carry
 
-    lax.fori_loop(0, CHUNKS, last_body, 0)
+    for chunk in range(CHUNKS):
+        last_body(chunk, 0)
 
 
 def filtered_and_applied(which, mixed, boundary):
@@ -124,41 +124,104 @@
     )(which, mixed, boundary)
 
 
-def per_device(orbitals, boundary, potential, trade):
-    own = lax.axis_index("d")
+def picked(source, values):
+    count = values.shape[0]
+    hot = lax.broadcasted_iota(jnp.int32, (count, count), 1) == source
+    hot = jnp.where(hot, 1.0, 0.0).astype(jnp.bfloat16)
+    return jnp.dot(hot, values, preferred_element_type=jnp.float32).astype(jnp.bfloat16)
+
+
+def product_kernel(core_ref, own_ref, other_ref, cols_ref, out_ref):
+    core = core_ref[0]
+    at = lax.broadcasted_iota(jnp.int32, (256, 256), 0)
+    z, xl, xh, c, r = at // 16, at // 8 % 2, at // 4 % 2, at // 2 % 2, at % 2
+    half = jnp.where(c == core, 0, 1)
+    rows = picked(
+        (((half * 2 + xl) * 2 + xh) * 16 + z) * 2 + r,
+        jnp.concatenate([own_ref[...], other_ref[...]], axis=0),
+    )
+    zh, which, y, zl, r = at // 64, at // 32 % 2, at // 8 % 4, at // 2 % 4, at % 2
+    cols = picked(((y * 16 + zh * 4 + zl) * 2 + which) * 2 + r, cols_ref[...])
+    block = lax.dot_general(
+        rows, cols, (((1,), (1,)), ((), ())), preferred_element_type=jnp.float32
+    )
+    for group in range(32):
+        for zh in range(4):
+            out_ref[group * 4 + zh] = block[8 * group : 8 * group + 8, 64 * zh : 64 * zh + 64]
+
+
+def block_product(core, own, other, cols):
+    whole = pl.BlockSpec(memory_space=pltpu.VMEM)
+    return pl.pallas_call(
+        product_kernel,
+        in_specs=[pl.BlockSpec(memory_space=pltpu.SMEM), whole, whole, whole],
+        out_specs=whole,
+        out_shape=jax.ShapeDtypeStruct((128, 8, 64), jnp.float32),
+        compiler_params=pltpu.CompilerParams(vmem_limit_bytes=32 * 1024 * 1024),
+        name="block_product",
+    )(core, own, other, cols)
+
+
+def finish_kernel(parts_ref, correlation_ref, projected_ref):
+    total = parts_ref[0]
+    for k in range(1, 16):
+        total = total + parts_ref[k]
+    total = total * (1.0 / (NZ * PLANE))
+    given = jnp.concatenate([total[k] for k in range(8)], axis=1)
+    at = lax.broadcasted_iota(jnp.int32, (512, 512), 1)
+    which, zl, y, xl, d, r = at // 256, at // 64 % 4, at // 16 % 4, at // 8 % 2, at // 2 % 4, at % 2
+    source = (xl * 4 + d) * 64 + ((which * 4 + y) * 4 + zl) * 2 + r
+    hot = jnp.where(lax.broadcasted_iota(jnp.int32, (512, 512), 0) == source, 1.0, 0.0)
+    placed = jnp.dot(
+        given, hot, preferred_element_type=jnp.float32, precision=lax.Precision.HIGHEST
+    )
+    correlation_ref[...] = placed[:, :256]
+    projected_ref[...] = placed[:, 256:]
+
+
+def finish(parts):
+    shape = jax.ShapeDtypeStruct((8, 256), jnp.float32)
+    whole = pl.BlockSpec(memory_space=pltpu.VMEM)
+    return pl.pallas_call(
+        finish_kernel,
+        in_specs=[whole],
+        out_specs=[whole, whole],
+        out_shape=[shape, shape],
+        name="finish",
+    )(parts)
+
+
+def per_device(orbitals, boundary, potential):
+    own = lax.axis_index("xh") * 2 + lax.axis_index("c")
     pieces = orbitals.reshape(4, 4, PLANE)
     pieces = jnp.concatenate([pieces, jnp.broadcast_to(potential[None], (4, 2, PLANE))], axis=1)
-    mixed = lax.all_to_all(pieces, "d", split_axis=0, concat_axis=0, tiled=True)
+    mixed = lax.all_to_all(pieces, ("xh", "c"), split_axis=0, concat_axis=0, tiled=True)
     fields = filtered_and_applied(
         own.astype(jnp.int32).reshape(1), mixed, boundary.reshape(4, 2, 4, PLANE)
     )
     shares = fields.reshape(4, SHARES, SHARE).transpose(1, 0, 2)
-    shares = lax.all_to_all(shares, ("y", "xl", "d"), split_axis=0, concat_axis=0, tiled=True)
-    shares = shares.reshape(SHARES, 2, 2, SHARE).transpose(1, 0, 2, 3).reshape(2, 64, SHARE)
-    columns = lax.all_gather(shares, "zl", axis=1, tiled=True).reshape(512, SHARE)
-    rows = lax.all_gather(shares[0], "zh", axis=0, tiled=True)
-    partial = lax.dot_general(
-        rows, columns, (((1,), (1,)), ((), ())), preferred_element_type=jnp.float32
-    )
-    partial = partial.reshape(4, 8, ORBS, 512).transpose(1, 0, 2, 3).reshape(SHARES, ORBS, 512)
-    parts = lax.all_to_all(partial, ("y", "xl", "d"), split_axis=0, concat_axis=0, tiled=True)
-    summed = jnp.sum(parts, axis=0) * (1.0 / (NZ * PLANE))
-    summed = lax.ppermute(summed, ("zh", "zl", "y", "xl", "d"), trade)
-    return summed[:, :256], summed[:, 256:]
+    shares = lax.all_to_all(shares, "z", split_axis=0, concat_axis=0, tiled=True)
+    cols = shares.reshape(4 * SHARES, SHARE)
+    cols = lax.all_to_all(
+        jnp.broadcast_to(cols[None], (4, 4 * SHARES, SHARE)), "y", split_axis=0, concat_axis=0, tiled=True
+    )
+    rows = shares[:, :2].reshape(2 * SHARES, SHARE)
+    rows = lax.all_gather(rows, ("xl", "xh"), axis=0, tiled=True)
+    other = lax.ppermute(rows, "c", [(0, 1), (1, 0)])
+    core = lax.axis_index("c").astype(jnp.int32).reshape(1)
+    partial = block_product(core, rows, other, cols.reshape(256, SHARE))
+    parts = lax.all_to_all(partial, ("z", "xl", "xh", "c"), split_axis=0, concat_axis=0, tiled=True)
+    correlation, projected = finish(parts.reshape(16, 8, 8, 64))
+    return correlation, projected
 
 
 def solution(mesh):
-    split = Mesh(mesh.devices.reshape(4, 4, 4, 2, 4), ("zh", "zl", "y", "xl", "d"))
-    trade = []
-    for zh in range(4):
-        for rest in range(32):
-            for d in range(4):
-                trade.append(((zh * 32 + rest) * 4 + d, (d * 32 + rest) * 4 + zh))
-    band = ("zh", "zl", "y", "xl")
+    split = Mesh(mesh.devices.reshape(16, 4, 2, 2, 2), ("z", "y", "xl", "xh", "c"))
+    band, domain = ("z", "y", "xl"), ("xh", "c")
     return jax.shard_map(
-        functools.partial(per_device, trade=trade),
+        per_device,
         mesh=split,
-        in_specs=(P(band, "d", None), P(band, None, None), P("d", None)),
-        out_specs=(P(band, "d"), P(band, "d")),
+        in_specs=(P(band, domain, None), P(band, None, None), P(domain, None)),
+        out_specs=(P(band, domain), P(band, domain)),
         check_vma=False,
     )

time: 146 us -> 122 us (0.84)
  waiting for transfers between devices: 30.5 us -> 7.14 us
  blocking collectives: 70.7 us -> 85.7 us
  between operations: 14.1 us -> 0.72 us
  starting transfers between devices: 13.3 us -> 11.2 us
  matrix products: 1.86 us -> 0 us
    all_to_all x2, blocking collectives: 33.6 us -> 70 us  [the longest x1 35.9 us: per_device(): lax.all_to_all(shares, 'z', split_axis=0, concat_axis=0, tiled=True)]
    all_gather x1, blocking collectives: 37.1 us -> 15.7 us  [per_device(): rows = lax.all_gather(rows, ('xl', 'xh'), axis=0, tiled=True)]
    all_gather x1 -> x0, waiting for transfers between devices: 17.2 us -> none  [per_device(): lax.all_gather(shares, 'zl', axis=1, tiled=True).reshape(512, SHARE)]
    ppermute x1, starting transfers between devices: 8.49 us -> 1.91 us  [per_device(): other = lax.ppermute(rows, 'c', [(0, 1), (1, 0)])]
    ppermute x1, waiting for transfers between devices: 8.25 us -> 2.06 us  [per_device(): other = lax.ppermute(rows, 'c', [(0, 1), (1, 0)])]
    pallas_call x1, Pallas kernels: 9.85 us -> 4.24 us  [filtered_and_applied(): pl.pallas_call(filter_kernel, grid_spec=pltpu.PrefetchScalarGridSpec(num_...]
    all_to_all x1 -> x2, starting transfers between devices: 4.83 us -> 9.29 us  [the longest x1 4.83 us: per_device(): lax.all_to_all(pieces, ('xh', 'c'), split_axis=0, concat_axis=0, tiled=True)]
    pallas_call x0 -> x2, Pallas kernels: none -> 4.17 us  [the longest x1 2.34 us: finish(): pl.pallas_call(finish_kernel, in_specs=[whole], out_specs=[whole, whole],...]
  transfers between devices with their start and end apart: 3 -> 3, of which waited for: 3 -> 2; matrix products, arithmetic and copies ran while one was open for 0% -> 0% of each run, Pallas kernels for 0% -> 0%
where the time goes in v2:
time: 122 us; the launch traced here: 121 us
  blocking collectives  85.7 us (70%)
  starting transfers between devices  11.2 us (9%)
  Pallas kernels  8.41 us (7%)
  waiting for transfers between devices  7.14 us (6%)
  local copies, waits for them, and re-layouts  5.35 us (4%)
  other arithmetic  2.14 us (2%)
    all_to_all x1, blocking collectives, per_device(): lax.all_to_all(shares, 'z', split_axis=0, concat_axis=0, tiled=True)  35.9 us
    all_to_all x1, blocking collectives, per_device(): lax.all_to_all(partial, ('z', 'xl', 'xh', 'c'), split_axis=0, concat_axis...  34 us
    all_gather x1, blocking collectives, per_device(): rows = lax.all_gather(rows, ('xl', 'xh'), axis=0, tiled=True)  15.7 us
    all_to_all x1, waiting for transfers between devices, per_device(): lax.all_to_all(pieces, ('xh', 'c'), split_axis=0, concat_axis=0, tiled=True)  5.08 us
    all_to_all x1, starting transfers between devices, per_device(): lax.all_to_all(pieces, ('xh', 'c'), split_axis=0, concat_axis=0, tiled=True)  4.83 us
    all_to_all x1, starting transfers between devices, per_device(): lax.all_to_all(jnp.broadcast_to(cols[None], (4, 4 * SHARES, SHARE)), 'y',...  4.46 us
    pallas_call x1, Pallas kernels, filtered_and_applied(): pl.pallas_call(filter_kernel, grid_spec=pltpu.PrefetchScalarGridSpec(num_...  4.24 us
  transfers between devices with their start and end apart: 3, of which 2 were waited for; matrix products, arithmetic and copies ran while one was open for 0% of the time, Pallas kernels for 0%

profile of v2, /device:TPU:6, one launch (start us, length us, event | category | flops | bytes accessed | tf_op | source)
XLA Modules:
  0.0 120.6 jit_solution(746589403272053846)
XLA Ops:
  0.6 0.0 copy-start
  0.6 1.0 reshape.32
  1.7 0.8 broadcast_in_dim.6
  2.4 0.9 pad_maximum_fusion
  3.3 4.8 %all-to-all-start = ((bf16[4,6,5120]{2,1,0:T(8,128)(2,1)}), bf16[4,6,5120]{2,1,0:T(8,128)(2,1)S(1)}, u32[]{:S(2)}, u32[]{:S(2)}) async-start(bf16[4,6,5120]{2,1,0:T(8,128)(2,1)} %pad_maximum_fusion), calls=%async_computation | async-start | bytes 655360 | tf_op jit(solution)/shard_map/all_to_all | solution.py:198
  8.2 5.1 %all-to-all-done.mixed_ref = bf16[4,6,5120]{2,1,0:T(8,128)(2,1)S(1)} async-done(((bf16[4,6,5120]{2,1,0:T(8,128)(2,1)}), bf16[4,6,5120]{2,1,0:T(8,128)(2,1)S(1)}, u32[]{:S(2)}, u32[]{:S(2)}) %all-to-all-start) | async-done | bytes 245792 | tf_op jit(solution)/shard_map/all_to_all | solution.py:198
  13.2 0.0 copy-done
  13.2 4.2 %chebyshev_filter.1 = bf16[4,8,5120]{2,1,0:T(8,128)(2,1)S(1)} custom-call(s32[1]{0:T(128)} %bitcast.1.which, bf16[4,6,5120]{2,1,0:T(8,128)(2,1)S(1)} %all-to-all-done.mixed_ref, bf16[4,2,4,5120]{3,2,1,0:T(4,128)(2,1)S(1)} %bitcast.9), custom_call_target="tpu_custom_call" | custom-call | tf_op jit(solution)/shard_map/chebyshev_filter/pallas_call | solution.py:104
  17.5 0.1 reshape.34
  17.6 0.3 copy.7
  17.9 35.9 %all_to_all.20 = bf16[16,4,2560]{2,1,0:T(4,128)(2,1)S(1)} all-to-all(bf16[16,4,2560]{2,1,0:T(4,128)(2,1)S(1)} %bitcast.11), channel_id=1, replica_groups=mesh['z'=16,'y'=4,'xl'=2,'xh'=2,'c'=2] {'z'}, dimensions={0} | all-to-all | bytes 655360 | tf_op jit(solution)/shard_map/all_to_all | solution.py:203
  53.8 0.1 broadcast_in_dim.14
  53.9 1.2 broadcast_in_dim.15
  55.1 4.5 %all-to-all-start.2 = ((bf16[4,64,2560]{2,1,0:T(8,128)(2,1)}), bf16[4,64,2560]{2,1,0:T(8,128)(2,1)S(1)}, u32[]{:S(2)}, u32[]{:S(2)}) async-start(bf16[4,64,2560]{2,1,0:T(8,128)(2,1)} %broadcast_in_dim.15), calls=%async_computation.2 | async-start | bytes 2621440 | tf_op jit(solution)/shard_map/all_to_all | solution.py:205
  59.5 0.1 slice.4
  59.6 0.1 reshape.35
  59.7 15.7 %all_gather.3.own_ref = bf16[128,2560]{1,0:T(8,128)(2,1)S(1)} all-gather(bf16[32,2560]{1,0:T(8,128)(2,1)S(1)} %reshape.35), channel_id=1, replica_groups=mesh['z'=16,'y'=4,'xl'=2,'xh'=2,'c'=2] {'xl','xh'}, dimensions={0}, use_global_device_ids=true | all-gather | bytes 819200 | tf_op jit(solution)/shard_map/all_gather | solution.py:209
  75.4 1.9 %collective-permute-start = (bf16[128,2560]{1,0:T(8,128)(2,1)S(1)}, bf16[128,2560]{1,0:T(8,128)(2,1)S(1)}, u32[]{:S(2)}, u32[]{:S(2)}) collective-permute-start(bf16[128,2560]{1,0:T(8,128)(2,1)S(1)} %all_gather.3.own_ref), channel_id=1, source_target_pairs={{0,1},{1,0},{2,3},{3,2},{4,5},{5,4},{6,7},{7,6},{8,9},{9,8},{10,11... | collective-permute-start | bytes 1966088 | tf_op jit(solution)/shard_map/ppermute | solution.py:210
  77.3 2.1 %collective-permute-done.other_ref = bf16[128,2560]{1,0:T(8,128)(2,1)S(1)} collective-permute-done((bf16[128,2560]{1,0:T(8,128)(2,1)S(1)}, bf16[128,2560]{1,0:T(8,128)(2,1)S(1)}, u32[]{:S(2)}, u32[]{:S(2)}) %collective-permute-start) | collective-permute-done | bytes 655392 | tf_op jit(solution)/shard_map/ppermute | solution.py:210
  79.4 0.0 all-to-all-done.2
  79.4 1.8 %block_product.1 = f32[128,8,64]{2,1,0:T(8,128)S(1)} custom-call(s32[1]{0:T(128)} %bitcast.core_ref, bf16[128,2560]{1,0:T(8,128)(2,1)S(1)} %all_gather.3.own_ref, bf16[128,2560]{1,0:T(8,128)(2,1)S(1)} %collective-permute-done.other_ref, bf16[256,2560]{1,0:T(8,128)(2,1)S(1)} %bitcast.8), custom_call_target="tpu_custom_call" | custom-call | tf_op jit(solution)/shard_map/block_product/pallas_call | solution.py:155
  81.2 0.3 reshape.38
  81.6 34.0 %all_to_all.21 = f32[128,1,512]{2,1,0:T(1,128)S(1)} all-to-all(f32[128,1,512]{2,1,0:T(1,128)S(1)} %reshape.38), channel_id=1, replica_groups=mesh['z'=16,'y'=4,'xl'=2,'xh'=2,'c'=2] {'z','xl','xh','c'}, dimensions={0} | all-to-all | bytes 524288 | tf_op jit(solution)/shard_map/all_to_all | solution.py:213
  115.6 0.5 broadcast.1
  116.1 1.3 %reduce = f32[128,512]{1,0:T(8,128)S(1)} reduce(f32[128,1,512]{2,1,0:T(1,128)S(1)} %all_to_all.21, f32[]{:T(128)} %broadcast.1), dimensions={1}, to_apply=%all_to_all.15.reduce_sub_computation | reduce | bytes 524292 | tf_op jit(solution)/shard_map/all_to_all | solution.py:213
  117.4 0.9 reshape.39
  118.3 2.3 %finish.1 = (f32[8,256]{1,0:T(8,128)}, f32[8,256]{1,0:T(8,128)}) custom-call(f32[16,8,8,64]{3,2,1,0:T(8,128)} %bitcast.10), custom_call_target="tpu_custom_call" | custom-call | tf_op jit(solution)/shard_map/finish/pallas_call | solution.py:185
Async XLA Ops:
  0.6 12.6 %copy-start = (bf16[8,4,5120]{2,1,0:T(4,128)(2,1)S(1)}, bf16[8,4,5120]{2,1,0:T(4,128)(2,1)}, u32[]{:S(2)}) copy-start(bf16[8,4,5120]{2,1,0:T(4,128)(2,1)} %param.4) | copy-start | bytes 983044
  3.3 9.9 %all-to-all-start = ((bf16[4,6,5120]{2,1,0:T(8,128)(2,1)}), bf16[4,6,5120]{2,1,0:T(8,128)(2,1)S(1)}, u32[]{:S(2)}, u32[]{:S(2)}) async-start(bf16[4,6,5120]{2,1,0:T(8,128)(2,1)} %pad_maximum_fusion), calls=%async_computation | async-start | bytes 655360 | tf_op jit(solution)/shard_map/all_to_all | solution.py:198
  55.1 24.4 %all-to-all-start.2 = ((bf16[4,64,2560]{2,1,0:T(8,128)(2,1)}), bf16[4,64,2560]{2,1,0:T(8,128)(2,1)S(1)}, u32[]{:S(2)}, u32[]{:S(2)}) async-start(bf16[4,64,2560]{2,1,0:T(8,128)(2,1)} %broadcast_in_dim.15), calls=%async_computation.2 | async-start | bytes 2621440 | tf_op jit(solution)/shard_map/all_to_all | solution.py:205
  75.4 4.0 %collective-permute-start = (bf16[128,2560]{1,0:T(8,128)(2,1)S(1)}, bf16[128,2560]{1,0:T(8,128)(2,1)S(1)}, u32[]{:S(2)}, u32[]{:S(2)}) collective-permute-start(bf16[128,2560]{1,0:T(8,128)(2,1)S(1)} %all_gather.3.own_ref), channel_id=1, source_target_pairs={{0,1},{1,0},{2,3},{3,2},{4,5},{5,4},{6,7},{7,6},{8,9},{9,8},{10,11... | collective-permute-start | bytes 1966088 | tf_op jit(solution)/shard_map/ppermute | solution.py:210

commit v3 on v2

--- a/solution.py
+++ b/solution.py
@@ -21,7 +21,6 @@
 
 
 def filter_kernel(which, mixed_ref, rim_ref, out_ref, one, two, rim_term, pot):
-    del which
     row = lax.broadcasted_iota(jnp.int32, (NZ, SPAN), 0)
     x = lax.rem(lax.broadcasted_iota(jnp.int32, (NZ, SPAN), 1), NX)
     zero = jnp.zeros((NZ, SPAN), jnp.float32)
@@ -36,12 +35,12 @@
         ref[orb, :, 0:PAD] = ref[orb, :, PLANE : PLANE + PAD]
         ref[orb, :, PAD + PLANE : 2 * PAD + PLANE] = ref[orb, :, PAD : 2 * PAD]
 
-    pot[...] = jnp.concatenate([mixed_ref[s, 4:6, :] for s in range(4)], axis=0).astype(jnp.float32)
+    pot[...] = jnp.concatenate([mixed_ref[s, 2] for s in range(4)], axis=0).astype(jnp.float32)
     for orb in range(2):
-        planes = [mixed_ref[s, 2 * orb : 2 * orb + 2, :] for s in range(4)]
+        planes = [mixed_ref[s, orb] for s in range(4)]
         one[orb, :, PAD : PAD + PLANE] = jnp.concatenate(planes, axis=0).astype(jnp.float32)
         wrap(one, orb)
-        rim = rim_ref[0, orb].astype(jnp.float32)
+        rim = rim_ref[which[0], orb].astype(jnp.float32)
         low_far, low, high, high_far = (rim[k : k + 1] for k in range(4))
         rim_term[orb] = jnp.concatenate(
             [16.0 * low - low_far, -low, jnp.zeros((4, PLANE), jnp.float32), -high, 16.0 * high - high_far],
@@ -101,53 +100,49 @@
 
 
 def filtered_and_applied(which, mixed, boundary):
+    whole = pl.BlockSpec(memory_space=pltpu.VMEM)
     return pl.pallas_call(
         filter_kernel,
-        grid_spec=pltpu.PrefetchScalarGridSpec(
-            num_scalar_prefetch=1,
-            grid=(1,),
-            in_specs=[
-                pl.BlockSpec((4, 6, PLANE), lambda i, which: (0, 0, 0)),
-                pl.BlockSpec((1, 2, 4, PLANE), lambda i, which: (which[0], 0, 0, 0)),
-            ],
-            out_specs=pl.BlockSpec((4, NZ, PLANE), lambda i, which: (0, 0, 0)),
-            scratch_shapes=[
-                pltpu.VMEM((2, NZ, PLANE + 2 * PAD), jnp.float32),
-                pltpu.VMEM((2, NZ, PLANE + 2 * PAD), jnp.float32),
-                pltpu.VMEM((2, NZ, PLANE), jnp.float32),
-                pltpu.VMEM((NZ, PLANE), jnp.float32),
-            ],
-        ),
+        in_specs=[pl.BlockSpec(memory_space=pltpu.SMEM), whole, whole],
+        out_specs=whole,
         out_shape=jax.ShapeDtypeStruct((4, NZ, PLANE), jnp.bfloat16),
+        scratch_shapes=[
+            pltpu.VMEM((2, NZ, PLANE + 2 * PAD), jnp.float32),
+            pltpu.VMEM((2, NZ, PLANE + 2 * PAD), jnp.float32),
+            pltpu.VMEM((2, NZ, PLANE), jnp.float32),
+            pltpu.VMEM((NZ, PLANE), jnp.float32),
+        ],
         compiler_params=pltpu.CompilerParams(vmem_limit_bytes=24 * 1024 * 1024),
         name="chebyshev_filter",
     )(which, mixed, boundary)
 
 
-def picked(source, values):
-    count = values.shape[0]
-    hot = lax.broadcasted_iota(jnp.int32, (count, count), 1) == source
-    hot = jnp.where(hot, 1.0, 0.0).astype(jnp.bfloat16)
-    return jnp.dot(hot, values, preferred_element_type=jnp.float32).astype(jnp.bfloat16)
-
-
-def product_kernel(core_ref, own_ref, other_ref, cols_ref, out_ref):
+def swapped(values):
+    return pltpu.roll(values, 64, 1)
+
+
+def product_kernel(core_ref, own_ref, other_ref, cols_ref, out_ref, blocks):
     core = core_ref[0]
-    at = lax.broadcasted_iota(jnp.int32, (256, 256), 0)
-    z, xl, xh, c, r = at // 16, at // 8 % 2, at // 4 % 2, at // 2 % 2, at % 2
-    half = jnp.where(c == core, 0, 1)
-    rows = picked(
-        (((half * 2 + xl) * 2 + xh) * 16 + z) * 2 + r,
-        jnp.concatenate([own_ref[...], other_ref[...]], axis=0),
-    )
-    zh, which, y, zl, r = at // 64, at // 32 % 2, at // 8 % 4, at // 2 % 4, at % 2
-    cols = picked(((y * 16 + zh * 4 + zl) * 2 + which) * 2 + r, cols_ref[...])
-    block = lax.dot_general(
-        rows, cols, (((1,), (1,)), ((), ())), preferred_element_type=jnp.float32
-    )
-    for group in range(32):
-        for zh in range(4):
-            out_ref[group * 4 + zh] = block[8 * group : 8 * group + 8, 64 * zh : 64 * zh + 64]
+    cols = jnp.concatenate(
+        [cols_ref[y, 16 * zh : 16 * zh + 16, :] for zh in range(4) for y in range(4)], axis=0
+    )
+    left = lax.broadcasted_iota(jnp.int32, (64, 128), 1) < 64
+    for rows_ref, place in ((own_ref, core), (other_ref, 1 - core)):
+        block = lax.dot_general(
+            rows_ref[...], cols, (((1,), (1,)), ((), ())), preferred_element_type=jnp.float32
+        )
+        for pair in range(2):
+            low = block[:64, 128 * pair : 128 * pair + 128]
+            high = block[64:, 128 * pair : 128 * pair + 128]
+            blocks[place, 2 * pair] = jnp.where(left, low, swapped(high))
+            blocks[place, 2 * pair + 1] = jnp.where(left, swapped(low), high)
+    for z in range(16):
+        for xl in range(2):
+            for zh in range(4):
+                for c in range(2):
+                    out_ref[(z * 2 + xl) * 4 + zh, 2 * c : 2 * c + 2, :] = blocks[
+                        c, zh, xl * 32 + z * 2 : xl * 32 + z * 2 + 2, :
+                    ]
 
 
 def block_product(core, own, other, cols):
@@ -156,25 +151,44 @@
         product_kernel,
         in_specs=[pl.BlockSpec(memory_space=pltpu.SMEM), whole, whole, whole],
         out_specs=whole,
-        out_shape=jax.ShapeDtypeStruct((128, 8, 64), jnp.float32),
-        compiler_params=pltpu.CompilerParams(vmem_limit_bytes=32 * 1024 * 1024),
+        out_shape=jax.ShapeDtypeStruct((128, 4, 128), jnp.float32),
+        scratch_shapes=[pltpu.VMEM((2, 4, 64, 128), jnp.float32)],
+        compiler_params=pltpu.CompilerParams(vmem_limit_bytes=24 * 1024 * 1024),
         name="block_product",
     )(core, own, other, cols)
 
 
 def finish_kernel(parts_ref, correlation_ref, projected_ref):
-    total = parts_ref[0]
-    for k in range(1, 16):
-        total = total + parts_ref[k]
-    total = total * (1.0 / (NZ * PLANE))
-    given = jnp.concatenate([total[k] for k in range(8)], axis=1)
-    at = lax.broadcasted_iota(jnp.int32, (512, 512), 1)
-    which, zl, y, xl, d, r = at // 256, at // 64 % 4, at // 16 % 4, at // 8 % 2, at // 2 % 4, at % 2
-    source = (xl * 4 + d) * 64 + ((which * 4 + y) * 4 + zl) * 2 + r
+    left = lax.broadcasted_iota(jnp.int32, (4, 128), 1) < 64
+    pieces = []
+    for pair in range(4):
+        one, two = parts_ref[2 * pair], parts_ref[2 * pair + 1]
+        for k in range(1, 16):
+            one = one + parts_ref[8 * k + 2 * pair]
+            two = two + parts_ref[8 * k + 2 * pair + 1]
+        low = jnp.where(left, one, swapped(two))
+        high = jnp.where(left, swapped(one), two)
+        pieces.append(jnp.concatenate([low, high], axis=0))
+    given = jnp.concatenate(pieces, axis=1) * (1.0 / (NZ * PLANE))
+    at = lax.broadcasted_iota(jnp.int32, (1, 512), 1)
+
+    def field(shift, count):
+        return lax.shift_right_logical(at, shift) & (count - 1)
+
+    group = field(3, 2) * 4 + field(1, 4)
+    source = group * 64 + field(4, 4) * 16 + field(6, 4) * 4 + field(8, 2) * 2 + field(0, 2)
     hot = jnp.where(lax.broadcasted_iota(jnp.int32, (512, 512), 0) == source, 1.0, 0.0)
+    top = given.astype(jnp.bfloat16)
+    rest = given - top.astype(jnp.float32)
+    middle = rest.astype(jnp.bfloat16)
+    last = (rest - middle.astype(jnp.float32)).astype(jnp.bfloat16)
+    split = jnp.concatenate(
+        [top.astype(jnp.float32), middle.astype(jnp.float32), last.astype(jnp.float32)], axis=0
+    )
     placed = jnp.dot(
-        given, hot, preferred_element_type=jnp.float32, precision=lax.Precision.HIGHEST
-    )
+        split.astype(jnp.bfloat16), hot.astype(jnp.bfloat16), preferred_element_type=jnp.float32
+    )
+    placed = (placed[16:] + placed[8:16]) + placed[:8]
     correlation_ref[...] = placed[:, :256]
     projected_ref[...] = placed[:, 256:]
 
@@ -193,8 +207,9 @@
 
 def per_device(orbitals, boundary, potential):
     own = lax.axis_index("xh") * 2 + lax.axis_index("c")
-    pieces = orbitals.reshape(4, 4, PLANE)
-    pieces = jnp.concatenate([pieces, jnp.broadcast_to(potential[None], (4, 2, PLANE))], axis=1)
+    pieces = jnp.concatenate(
+        [orbitals.reshape(4, 2, 2, PLANE), jnp.broadcast_to(potential, (4, 1, 2, PLANE))], axis=1
+    )
     mixed = lax.all_to_all(pieces, ("xh", "c"), split_axis=0, concat_axis=0, tiled=True)
     fields = filtered_and_applied(
         own.astype(jnp.int32).reshape(1), mixed, boundary.reshape(4, 2, 4, PLANE)
@@ -206,13 +221,12 @@
         jnp.broadcast_to(cols[None], (4, 4 * SHARES, SHARE)), "y", split_axis=0, concat_axis=0, tiled=True
     )
     rows = shares[:, :2].reshape(2 * SHARES, SHARE)
-    rows = lax.all_gather(rows, ("xl", "xh"), axis=0, tiled=True)
+    rows = lax.all_gather(rows, ("xh", "xl"), axis=0, tiled=True)
     other = lax.ppermute(rows, "c", [(0, 1), (1, 0)])
     core = lax.axis_index("c").astype(jnp.int32).reshape(1)
-    partial = block_product(core, rows, other, cols.reshape(256, SHARE))
+    partial = block_product(core, rows, other, cols)
     parts = lax.all_to_all(partial, ("z", "xl", "xh", "c"), split_axis=0, concat_axis=0, tiled=True)
-    correlation, projected = finish(parts.reshape(16, 8, 8, 64))
-    return correlation, projected
+    return tuple(finish(parts))
 
 
 def solution(mesh):

time: 122 us -> 114 us (0.934)
  local copies, waits for them, and re-layouts: 5.35 us -> 2.62 us
  blocking collectives: 85.7 us -> 83 us
    all_gather x1, blocking collectives: 15.7 us -> 13 us  [per_device(): rows = lax.all_gather(rows, ('xh', 'xl'), axis=0, tiled=True)]
    all_to_all x1 -> x0, other arithmetic: 1.26 us -> none  [per_device(): lax.all_to_all(partial, ('z', 'xl', 'xh', 'c'), split_axis=0, concat_axis...]
    unnamed x4 -> x2, local copies, waits for them, and re-layouts: 1.25 us -> 0.01 us
where the time goes in v3:
time: 114 us; the launch traced here: 113 us
  blocking collectives  83 us (73%)
  starting transfers between devices  11.2 us (10%)
  Pallas kernels  7.21 us (6%)
  waiting for transfers between devices  6.27 us (6%)
  local copies, waits for them, and re-layouts  2.62 us (2%)
  other arithmetic  1.93 us (2%)
    all_to_all x1, blocking collectives, per_device(): lax.all_to_all(shares, 'z', split_axis=0, concat_axis=0, tiled=True)  36 us
    all_to_all x1, blocking collectives, per_device(): lax.all_to_all(partial, ('z', 'xl', 'xh', 'c'), split_axis=0, concat_axis...  34 us
    all_gather x1, blocking collectives, per_device(): rows = lax.all_gather(rows, ('xh', 'xl'), axis=0, tiled=True)  13 us
    all_to_all x1, starting transfers between devices, per_device(): lax.all_to_all(pieces, ('xh', 'c'), split_axis=0, concat_axis=0, tiled=True)  4.8 us
    all_to_all x1, starting transfers between devices, per_device(): lax.all_to_all(jnp.broadcast_to(cols[None], (4, 4 * SHARES, SHARE)), 'y',...  4.46 us
    pallas_call x1, Pallas kernels, filtered_and_applied(): pl.pallas_call(filter_kernel, in_specs=[pl.BlockSpec(memory_space=pltpu.S...  4.24 us
    all_to_all x1, waiting for transfers between devices, per_device(): lax.all_to_all(pieces, ('xh', 'c'), split_axis=0, concat_axis=0, tiled=True)  4.2 us
  transfers between devices with their start and end apart: 3, of which 2 were waited for; matrix products, arithmetic and copies ran while one was open for 0% of the time, Pallas kernels for 0%

profile of v3, /device:TPU:6, one launch (start us, length us, event | category | flops | bytes accessed | tf_op | source)
XLA Modules:
  0.0 112.9 jit_solution(7164689694672188352)
XLA Ops:
  0.6 0.0 copy-start
  0.6 0.8 broadcast_in_dim.10
  1.5 1.9 %pad_maximum_fusion = bf16[4,3,2,5120]{3,2,1,0:T(2,128)(2,1)} fusion(bf16[4,1,2,5120]{3,2,1,0:T(2,128)(2,1)S(1)} %broadcast_in_dim.10, bf16[4,2,2,5120]{3,2,1,0:T(2,128)(2,1)} %bitcast.9), kind=kLoop, calls=%fused_computation.1 | loop fusion | flops 122880 | bytes 491520 | tf_op jit(solution)/shard_map/concatenate | solution.py:210
  3.4 4.8 %all-to-all-start = ((bf16[4,3,2,5120]{3,2,1,0:T(2,128)(2,1)}), bf16[4,3,2,5120]{3,2,1,0:T(2,128)(2,1)S(1)}, u32[]{:S(2)}, u32[]{:S(2)}) async-start(bf16[4,3,2,5120]{3,2,1,0:T(2,128)(2,1)} %pad_maximum_fusion), calls=%async_computation | async-start | bytes 491520 | tf_op jit(solution)/shard_map/all_to_all | solution.py:213
  8.2 4.2 %all-to-all-done.mixed_ref = bf16[4,3,2,5120]{3,2,1,0:T(2,128)(2,1)S(1)} async-done(((bf16[4,3,2,5120]{3,2,1,0:T(2,128)(2,1)}), bf16[4,3,2,5120]{3,2,1,0:T(2,128)(2,1)S(1)}, u32[]{:S(2)}, u32[]{:S(2)}) %all-to-all-start) | async-done | bytes 245792 | tf_op jit(solution)/shard_map/all_to_all | solution.py:213
  12.4 0.0 copy-done
  12.4 4.2 %chebyshev_filter.1 = bf16[4,8,5120]{2,1,0:T(8,128)(2,1)S(1)} custom-call(s32[1]{0:T(128)} %bitcast.1.which, bf16[4,3,2,5120]{3,2,1,0:T(2,128)(2,1)S(1)} %all-to-all-done.mixed_ref, bf16[4,2,4,5120]{3,2,1,0:T(4,128)(2,1)S(1)} %bitcast.7), custom_call_target="tpu_custom_call" | custom-call | tf_op jit(solution)/shard_map/chebyshev_filter/pallas_call | solution.py:104
  16.6 0.1 reshape.27
  16.8 0.3 copy.7
  17.0 36.0 %all_to_all.20 = bf16[16,4,2560]{2,1,0:T(4,128)(2,1)S(1)} all-to-all(bf16[16,4,2560]{2,1,0:T(4,128)(2,1)S(1)} %bitcast.8), channel_id=1, replica_groups=mesh['z'=16,'y'=4,'xl'=2,'xh'=2,'c'=2] {'z'}, dimensions={0} | all-to-all | bytes 655360 | tf_op jit(solution)/shard_map/all_to_all | solution.py:218
  53.0 0.1 broadcast_in_dim.11
  53.1 1.2 %broadcast_in_dim.12 = bf16[4,64,2560]{2,1,0:T(8,128)(2,1)} broadcast(bf16[64,2560]{1,0:T(8,128)(2,1)S(1)} %broadcast_in_dim.11), dimensions={1,2} | broadcast | bytes 1638400 | tf_op jit(solution)/shard_map/broadcast_in_dim | solution.py:221
  54.2 4.5 %all-to-all-start.2 = ((bf16[4,64,2560]{2,1,0:T(8,128)(2,1)}), bf16[4,64,2560]{2,1,0:T(8,128)(2,1)S(1)}, u32[]{:S(2)}, u32[]{:S(2)}) async-start(bf16[4,64,2560]{2,1,0:T(8,128)(2,1)} %broadcast_in_dim.12), calls=%async_computation.2 | async-start | bytes 2621440 | tf_op jit(solution)/shard_map/all_to_all | solution.py:220
  58.7 0.1 slice.4
  58.8 0.1 reshape.28
  58.9 13.0 %all_gather.3.own_ref = bf16[128,2560]{1,0:T(8,128)(2,1)S(1)} all-gather(bf16[32,2560]{1,0:T(8,128)(2,1)S(1)} %reshape.28), channel_id=1, replica_groups=mesh['z'=16,'y'=4,'xl'=2,'xh'=2,'c'=2] {'xh','xl'}, dimensions={0}, use_global_device_ids=true | all-gather | bytes 819200 | tf_op jit(solution)/shard_map/all_gather | solution.py:224
  71.9 1.9 %collective-permute-start = (bf16[128,2560]{1,0:T(8,128)(2,1)S(1)}, bf16[128,2560]{1,0:T(8,128)(2,1)S(1)}, u32[]{:S(2)}, u32[]{:S(2)}) collective-permute-start(bf16[128,2560]{1,0:T(8,128)(2,1)S(1)} %all_gather.3.own_ref), channel_id=1, source_target_pairs={{0,1},{1,0},{2,3},{3,2},{4,5},{5,4},{6,7},{7,6},{8,9},{9,8},{10,11... | collective-permute-start | bytes 1966088 | tf_op jit(solution)/shard_map/ppermute | solution.py:225
  73.9 2.1 %collective-permute-done.other_ref = bf16[128,2560]{1,0:T(8,128)(2,1)S(1)} collective-permute-done((bf16[128,2560]{1,0:T(8,128)(2,1)S(1)}, bf16[128,2560]{1,0:T(8,128)(2,1)S(1)}, u32[]{:S(2)}, u32[]{:S(2)}) %collective-permute-start) | collective-permute-done | bytes 655392 | tf_op jit(solution)/shard_map/ppermute | solution.py:225
  75.9 0.0 all-to-all-done.2.cols_ref
  75.9 1.2 %block_product.1 = f32[128,4,128]{2,1,0:T(4,128)S(1)} custom-call(s32[1]{0:T(128)} %bitcast.core_ref, bf16[128,2560]{1,0:T(8,128)(2,1)S(1)} %all_gather.3.own_ref, bf16[128,2560]{1,0:T(8,128)(2,1)S(1)} %collective-permute-done.other_ref, bf16[4,64,2560]{2,1,0:T(8,128)(2,1)S(1)} %all-to-all-done.2.cols_ref), custom_call_target="tpu_custom_call" | custom-call | tf_op jit(solution)/shard_map/block_product/pallas_call | solution.py:150
  77.1 34.0 %all_to_all.21.parts_ref = f32[128,4,128]{2,1,0:T(4,128)} all-to-all(f32[128,4,128]{2,1,0:T(4,128)S(1)} %block_product.1), channel_id=1, replica_groups=mesh['z'=16,'y'=4,'xl'=2,'xh'=2,'c'=2] {'z','xl','xh','c'}, dimensions={0} | all-to-all | bytes 524288 | tf_op jit(solution)/shard_map/all_to_all | solution.py:228
  111.1 1.8 %finish.1 = (f32[8,256]{1,0:T(8,128)}, f32[8,256]{1,0:T(8,128)}) custom-call(f32[128,4,128]{2,1,0:T(4,128)} %all_to_all.21.parts_ref), custom_call_target="tpu_custom_call" | custom-call | tf_op jit(solution)/shard_map/finish/pallas_call | solution.py:199
Async XLA Ops:
  0.6 11.8 %copy-start = (bf16[8,4,5120]{2,1,0:T(4,128)(2,1)S(1)}, bf16[8,4,5120]{2,1,0:T(4,128)(2,1)}, u32[]{:S(2)}) copy-start(bf16[8,4,5120]{2,1,0:T(4,128)(2,1)} %param.4) | copy-start | bytes 983044
  3.4 9.0 %all-to-all-start = ((bf16[4,3,2,5120]{3,2,1,0:T(2,128)(2,1)}), bf16[4,3,2,5120]{3,2,1,0:T(2,128)(2,1)S(1)}, u32[]{:S(2)}, u32[]{:S(2)}) async-start(bf16[4,3,2,5120]{3,2,1,0:T(2,128)(2,1)} %pad_maximum_fusion), calls=%async_computation | async-start | bytes 491520 | tf_op jit(solution)/shard_map/all_to_all | solution.py:213
  54.2 21.7 %all-to-all-start.2 = ((bf16[4,64,2560]{2,1,0:T(8,128)(2,1)}), bf16[4,64,2560]{2,1,0:T(8,128)(2,1)S(1)}, u32[]{:S(2)}, u32[]{:S(2)}) async-start(bf16[4,64,2560]{2,1,0:T(8,128)(2,1)} %broadcast_in_dim.12), calls=%async_computation.2 | async-start | bytes 2621440 | tf_op jit(solution)/shard_map/all_to_all | solution.py:220
  71.9 4.0 %collective-permute-start = (bf16[128,2560]{1,0:T(8,128)(2,1)S(1)}, bf16[128,2560]{1,0:T(8,128)(2,1)S(1)}, u32[]{:S(2)}, u32[]{:S(2)}) collective-permute-start(bf16[128,2560]{1,0:T(8,128)(2,1)S(1)} %all_gather.3.own_ref), channel_id=1, source_target_pairs={{0,1},{1,0},{2,3},{3,2},{4,5},{5,4},{6,7},{7,6},{8,9},{9,8},{10,11... | collective-permute-start | bytes 1966088 | tf_op jit(solution)/shard_map/ppermute | solution.py:225

commit v4 on v3

--- a/solution.py
+++ b/solution.py
@@ -20,47 +20,78 @@
 filter_radius = 4.5
 
 
-def filter_kernel(which, mixed_ref, rim_ref, out_ref, one, two, rim_term, pot):
-    row = lax.broadcasted_iota(jnp.int32, (NZ, SPAN), 0)
-    x = lax.rem(lax.broadcasted_iota(jnp.int32, (NZ, SPAN), 1), NX)
-    zero = jnp.zeros((NZ, SPAN), jnp.float32)
-    below_1 = jnp.where(row >= 1, zero + 16.0, zero)
-    above_1 = jnp.where(row <= NZ - 2, zero + 16.0, zero)
-    below_2 = jnp.where(row >= 2, zero + 1.0, zero)
-    above_2 = jnp.where(row <= NZ - 3, zero + 1.0, zero)
-    first, last = x == 0, x == NX - 1
-    first_two, last_two = x <= 1, x >= NX - 2
-
-    def wrap(ref, orb):
-        ref[orb, :, 0:PAD] = ref[orb, :, PLANE : PLANE + PAD]
-        ref[orb, :, PAD + PLANE : 2 * PAD + PLANE] = ref[orb, :, PAD : 2 * PAD]
-
-    pot[...] = jnp.concatenate([mixed_ref[s, 2] for s in range(4)], axis=0).astype(jnp.float32)
+def prepare_kernel(which, rim_ref, rim_term, hot_ref):
     for orb in range(2):
-        planes = [mixed_ref[s, orb] for s in range(4)]
-        one[orb, :, PAD : PAD + PLANE] = jnp.concatenate(planes, axis=0).astype(jnp.float32)
-        wrap(one, orb)
         rim = rim_ref[which[0], orb].astype(jnp.float32)
         low_far, low, high, high_far = (rim[k : k + 1] for k in range(4))
         rim_term[orb] = jnp.concatenate(
             [16.0 * low - low_far, -low, jnp.zeros((4, PLANE), jnp.float32), -high, 16.0 * high - high_far],
             axis=0,
         )
+    at = lax.broadcasted_iota(jnp.int32, (1, 512), 1)
+
+    def field(shift, count):
+        return lax.shift_right_logical(at, shift) & (count - 1)
+
+    group = field(3, 2) * 4 + field(1, 4)
+    source = group * 64 + field(4, 4) * 16 + field(6, 4) * 4 + field(8, 2) * 2 + field(0, 2)
+    hot = jnp.where(lax.broadcasted_iota(jnp.int32, (512, 512), 0) == source, 1.0, 0.0)
+    hot_ref[...] = hot.astype(jnp.bfloat16)
+
+
+def prepared(which, boundary):
+    whole = pl.BlockSpec(memory_space=pltpu.VMEM)
+    return pl.pallas_call(
+        prepare_kernel,
+        in_specs=[pl.BlockSpec(memory_space=pltpu.SMEM), whole],
+        out_specs=[whole, whole],
+        out_shape=[
+            jax.ShapeDtypeStruct((2, NZ, PLANE), jnp.float32),
+            jax.ShapeDtypeStruct((512, 512), jnp.bfloat16),
+        ],
+        name="prepare",
+    )(which, boundary)
+
+
+def filter_kernel(mixed_ref, rim_term, out_ref, one, two, pot):
+    row = lax.broadcasted_iota(jnp.int32, (NZ, SPAN), 0)
+    zero = jnp.zeros((NZ, SPAN), jnp.float32)
+    below_1 = jnp.where(row >= 1, zero + 16.0, zero)
+    above_1 = jnp.where(row <= NZ - 2, zero + 16.0, zero)
+    below_2 = jnp.where(row >= 2, zero + 1.0, zero)
+    above_2 = jnp.where(row <= NZ - 3, zero + 1.0, zero)
+    width = SPAN + 2 * PAD
+    x = lax.rem(lax.broadcasted_iota(jnp.int32, (NZ, width), 1) + (3 * NX - PAD), NX)
+    first, last = x == 0, x == NX - 1
+    first_two, last_two = x <= 1, x >= NX - 2
+
+    def wrap(ref, orb):
+        ref[orb, :, 0:PAD] = ref[orb, :, PLANE : PLANE + PAD]
+        ref[orb, :, PAD + PLANE : 2 * PAD + PLANE] = ref[orb, :, PAD : 2 * PAD]
+
+    pot[...] = jnp.concatenate([mixed_ref[s, 2] for s in range(4)], axis=0).astype(jnp.float32)
+    for orb in range(2):
+        planes = [mixed_ref[s, orb] for s in range(4)]
+        one[orb, :, PAD : PAD + PLANE] = jnp.concatenate(planes, axis=0).astype(jnp.float32)
+        wrap(one, orb)
 
     def apply_ham(ref, orb, at):
         window = ref[orb, :, pl.ds(at, SPAN + 2 * PAD)]
-        width = SPAN + 2 * PAD
-
-        def cells(shift):
-            return pltpu.roll(window, (-shift) % width, 1)[:, PAD : PAD + SPAN]
-
-        middle = window[:, PAD : PAD + SPAN]
-        near = jnp.where(first, cells(NX - 1), cells(-1)) + jnp.where(last, cells(1 - NX), cells(1))
-        near = near + (cells(NX) + cells(-NX))
-        far = jnp.where(first_two, cells(NX - 2), cells(-2)) + jnp.where(
-            last_two, cells(2 - NX), cells(2)
-        )
-        far = far + (cells(2 * NX) + cells(-2 * NX))
+
+        def moved(values, shift):
+            return pltpu.roll(values, (-shift) % width, 1)
+
+        def inner(values):
+            return values[:, PAD : PAD + SPAN]
+
+        middle = inner(window)
+        up, down = moved(window, NX), moved(window, -NX)
+        near = inner(moved(jnp.where(last, up, window), -1))
+        near = near + inner(moved(jnp.where(first, down, window), 1))
+        near = near + (inner(up) + inner(down))
+        far = inner(moved(jnp.where(last_two, up, window), -2))
+        far = far + inner(moved(jnp.where(first_two, down, window), 2))
+        far = far + (inner(moved(window, 2 * NX)) + inner(moved(window, -2 * NX)))
         z_near = below_1 * pltpu.roll(middle, 1, 0) + above_1 * pltpu.roll(middle, NZ - 1, 0)
         z_far = below_2 * pltpu.roll(middle, 2, 0) + above_2 * pltpu.roll(middle, NZ - 2, 0)
         total = (16.0 * near - far) + (z_near - z_far) - 90.0 * middle
@@ -99,22 +130,21 @@
         last_body(chunk, 0)
 
 
-def filtered_and_applied(which, mixed, boundary):
+def filtered_and_applied(mixed, rim_term):
     whole = pl.BlockSpec(memory_space=pltpu.VMEM)
     return pl.pallas_call(
         filter_kernel,
-        in_specs=[pl.BlockSpec(memory_space=pltpu.SMEM), whole, whole],
+        in_specs=[whole, whole],
         out_specs=whole,
         out_shape=jax.ShapeDtypeStruct((4, NZ, PLANE), jnp.bfloat16),
         scratch_shapes=[
             pltpu.VMEM((2, NZ, PLANE + 2 * PAD), jnp.float32),
             pltpu.VMEM((2, NZ, PLANE + 2 * PAD), jnp.float32),
-            pltpu.VMEM((2, NZ, PLANE), jnp.float32),
             pltpu.VMEM((NZ, PLANE), jnp.float32),
         ],
         compiler_params=pltpu.CompilerParams(vmem_limit_bytes=24 * 1024 * 1024),
         name="chebyshev_filter",
-    )(which, mixed, boundary)
+    )(mixed, rim_term)
 
 
 def swapped(values):
@@ -158,7 +188,7 @@
     )(core, own, other, cols)
 
 
-def finish_kernel(parts_ref, correlation_ref, projected_ref):
+def finish_kernel(parts_ref, hot_ref, correlation_ref, projected_ref):
     left = lax.broadcasted_iota(jnp.int32, (4, 128), 1) < 64
     pieces = []
     for pair in range(4):
@@ -170,14 +200,6 @@
         high = jnp.where(left, swapped(one), two)
         pieces.append(jnp.concatenate([low, high], axis=0))
     given = jnp.concatenate(pieces, axis=1) * (1.0 / (NZ * PLANE))
-    at = lax.broadcasted_iota(jnp.int32, (1, 512), 1)
-
-    def field(shift, count):
-        return lax.shift_right_logical(at, shift) & (count - 1)
-
-    group = field(3, 2) * 4 + field(1, 4)
-    source = group * 64 + field(4, 4) * 16 + field(6, 4) * 4 + field(8, 2) * 2 + field(0, 2)
-    hot = jnp.where(lax.broadcasted_iota(jnp.int32, (512, 512), 0) == source, 1.0, 0.0)
     top = given.astype(jnp.bfloat16)
     rest = given - top.astype(jnp.float32)
     middle = rest.astype(jnp.bfloat16)
@@ -185,35 +207,52 @@
     split = jnp.concatenate(
         [top.astype(jnp.float32), middle.astype(jnp.float32), last.astype(jnp.float32)], axis=0
     )
-    placed = jnp.dot(
-        split.astype(jnp.bfloat16), hot.astype(jnp.bfloat16), preferred_element_type=jnp.float32
-    )
+    placed = jnp.dot(split.astype(jnp.bfloat16), hot_ref[...], preferred_element_type=jnp.float32)
     placed = (placed[16:] + placed[8:16]) + placed[:8]
     correlation_ref[...] = placed[:, :256]
     projected_ref[...] = placed[:, 256:]
 
 
-def finish(parts):
+def finish(parts, hot):
     shape = jax.ShapeDtypeStruct((8, 256), jnp.float32)
     whole = pl.BlockSpec(memory_space=pltpu.VMEM)
     return pl.pallas_call(
         finish_kernel,
-        in_specs=[whole],
+        in_specs=[whole, whole],
         out_specs=[whole, whole],
         out_shape=[shape, shape],
         name="finish",
-    )(parts)
+    )(parts, hot)
+
+
+def pieces_kernel(orbitals_ref, potential_ref, out_ref, sems):
+    copies = [pltpu.make_async_copy(orbitals_ref, out_ref.at[:, 0:2], sems.at[0])]
+    for k in range(4):
+        copies.append(pltpu.make_async_copy(potential_ref, out_ref.at[k, 2], sems.at[1 + k]))
+    for copy in copies:
+        copy.start()
+    for copy in copies:
+        copy.wait()
+
+
+def pieces_of(orbitals, potential):
+    anywhere = pl.BlockSpec(memory_space=pl.ANY)
+    return pl.pallas_call(
+        pieces_kernel,
+        in_specs=[anywhere, anywhere],
+        out_specs=anywhere,
+        out_shape=jax.ShapeDtypeStruct((4, 3, 2, PLANE), jnp.bfloat16),
+        scratch_shapes=[pltpu.SemaphoreType.DMA((5,))],
+        name="pieces",
+    )(orbitals, potential)
 
 
 def per_device(orbitals, boundary, potential):
     own = lax.axis_index("xh") * 2 + lax.axis_index("c")
-    pieces = jnp.concatenate(
-        [orbitals.reshape(4, 2, 2, PLANE), jnp.broadcast_to(potential, (4, 1, 2, PLANE))], axis=1
-    )
+    pieces = pieces_of(orbitals.reshape(4, 2, 2, PLANE), potential)
     mixed = lax.all_to_all(pieces, ("xh", "c"), split_axis=0, concat_axis=0, tiled=True)
-    fields = filtered_and_applied(
-        own.astype(jnp.int32).reshape(1), mixed, boundary.reshape(4, 2, 4, PLANE)
-    )
+    rim_term, hot = prepared(own.astype(jnp.int32).reshape(1), boundary.reshape(4, 2, 4, PLANE))
+    fields = filtered_and_applied(mixed, rim_term)
     shares = fields.reshape(4, SHARES, SHARE).transpose(1, 0, 2)
     shares = lax.all_to_all(shares, "z", split_axis=0, concat_axis=0, tiled=True)
     cols = shares.reshape(4 * SHARES, SHARE)
@@ -226,7 +265,7 @@
     core = lax.axis_index("c").astype(jnp.int32).reshape(1)
     partial = block_product(core, rows, other, cols)
     parts = lax.all_to_all(partial, ("z", "xl", "xh", "c"), split_axis=0, concat_axis=0, tiled=True)
-    return tuple(finish(parts))
+    return tuple(finish(parts, hot))
 
 
 def solution(mesh):

time: 114 us -> 125 us (1.096)
  Pallas kernels: 7.21 us -> 21.7 us
  waiting for transfers between devices: 6.27 us -> 4.26 us
  other arithmetic: 1.93 us -> 0 us
    pallas_call x2 -> x4, Pallas kernels: 6.06 us -> 20.6 us  [the longest x1 8.59 us: pieces_of(): pl.pallas_call(pieces_kernel, in_specs=[anywhere, anywhere], out_specs=an...]
    all_to_all x1, waiting for transfers between devices: 4.2 us -> 2.19 us  [per_device(): lax.all_to_all(pieces, ('xh', 'c'), split_axis=0, concat_axis=0, tiled=True)]
    concatenate x1 -> x0, other arithmetic: 1.93 us -> none  [per_device(): jnp.concatenate([orbitals.reshape(4, 2, 2, PLANE), jnp.broadcast_to(poten...]
  transfers between devices with their start and end apart: 3 -> 3, of which waited for: 2 -> 2; matrix products, arithmetic and copies ran while one was open for 0% -> 0% of each run, Pallas kernels for 0% -> 2%
where the time goes in v4:
time: 125 us; the launch traced here: 124 us
  blocking collectives  83 us (66%)
  Pallas kernels  21.7 us (17%)
  starting transfers between devices  11.2 us (9%)
  waiting for transfers between devices  4.26 us (3%)
  local copies, waits for them, and re-layouts  2.78 us (2%)
    all_to_all x1, blocking collectives, per_device(): lax.all_to_all(shares, 'z', split_axis=0, concat_axis=0, tiled=True)  36 us
    all_to_all x1, blocking collectives, per_device(): lax.all_to_all(partial, ('z', 'xl', 'xh', 'c'), split_axis=0, concat_axis...  34 us
    all_gather x1, blocking collectives, per_device(): rows = lax.all_gather(rows, ('xh', 'xl'), axis=0, tiled=True)  13 us
    pallas_call x1, Pallas kernels, pieces_of(): pl.pallas_call(pieces_kernel, in_specs=[anywhere, anywhere], out_specs=an...  8.59 us
    pallas_call x1, Pallas kernels, filtered_and_applied(): pl.pallas_call(filter_kernel, in_specs=[whole, whole], out_specs=whole, o...  7.98 us
    all_to_all x1, starting transfers between devices, per_device(): lax.all_to_all(pieces, ('xh', 'c'), split_axis=0, concat_axis=0, tiled=True)  4.81 us
    all_to_all x1, starting transfers between devices, per_device(): lax.all_to_all(jnp.broadcast_to(cols[None], (4, 4 * SHARES, SHARE)), 'y',...  4.46 us
  transfers between devices with their start and end apart: 3, of which 2 were waited for; matrix products, arithmetic and copies ran while one was open for 0% of the time, Pallas kernels for 2%

profile of v4, /device:TPU:6, one launch (start us, length us, event | category | flops | bytes accessed | tf_op | source)
XLA Modules:
  0.0 123.6 jit_solution(12010987463296876024)
XLA Ops:
  0.6 8.6 %pieces.1 = bf16[4,3,2,5120]{3,2,1,0:T(2,128)(2,1)} custom-call(bf16[4,2,2,5120]{3,2,1,0:T(2,128)(2,1)} %bitcast.9, bf16[2,5120]{1,0:T(2,128)(2,1)} %potential_ref.1), custom_call_target="tpu_custom_call" | custom-call | tf_op jit(solution)/shard_map/pieces/pallas_call | solution.py:240
  9.2 4.8 %all-to-all-start = ((bf16[4,3,2,5120]{3,2,1,0:T(2,128)(2,1)}), bf16[4,3,2,5120]{3,2,1,0:T(2,128)(2,1)S(1)}, u32[]{:S(2)}, u32[]{:S(2)}) async-start(bf16[4,3,2,5120]{3,2,1,0:T(2,128)(2,1)} %pieces.1), calls=%async_computation | async-start | bytes 491520 | tf_op jit(solution)/shard_map/all_to_all | solution.py:253
  14.0 2.0 %prepare.1 = (f32[2,8,5120]{2,1,0:T(8,128)}, bf16[512,512]{1,0:T(8,128)(2,1)}) custom-call(s32[1]{0:T(128)} %bitcast.2.which, bf16[4,2,4,5120]{3,2,1,0:T(4,128)(2,1)} %bitcast.8), custom_call_target="tpu_custom_call" | custom-call | tf_op jit(solution)/shard_map/prepare/pallas_call | solution.py:44
  16.0 2.2 %all-to-all-done.mixed_ref = bf16[4,3,2,5120]{3,2,1,0:T(2,128)(2,1)S(1)} async-done(((bf16[4,3,2,5120]{3,2,1,0:T(2,128)(2,1)}), bf16[4,3,2,5120]{3,2,1,0:T(2,128)(2,1)S(1)}, u32[]{:S(2)}, u32[]{:S(2)}) %all-to-all-start) | async-done | bytes 245792 | tf_op jit(solution)/shard_map/all_to_all | solution.py:253
  18.2 0.0 copy-start
  18.2 1.0 copy-done
  19.2 8.0 %chebyshev_filter.1 = bf16[4,8,5120]{2,1,0:T(8,128)(2,1)S(1)} custom-call(bf16[4,3,2,5120]{3,2,1,0:T(2,128)(2,1)S(1)} %all-to-all-done.mixed_ref, f32[2,8,5120]{2,1,0:T(8,128)S(1)} %copy-done), custom_call_target="tpu_custom_call" | custom-call | tf_op jit(solution)/shard_map/chebyshev_filter/pallas_call | solution.py:135
  27.2 0.1 reshape.27
  27.3 0.3 copy.7
  27.6 36.0 %all_to_all.20 = bf16[16,4,2560]{2,1,0:T(4,128)(2,1)S(1)} all-to-all(bf16[16,4,2560]{2,1,0:T(4,128)(2,1)S(1)} %bitcast.7), channel_id=1, replica_groups=mesh['z'=16,'y'=4,'xl'=2,'xh'=2,'c'=2] {'z'}, dimensions={0} | all-to-all | bytes 655360 | tf_op jit(solution)/shard_map/all_to_all | solution.py:257
  63.6 0.1 broadcast_in_dim.7
  63.6 1.2 broadcast_in_dim.8
  64.8 4.5 %all-to-all-start.2 = ((bf16[4,64,2560]{2,1,0:T(8,128)(2,1)}), bf16[4,64,2560]{2,1,0:T(8,128)(2,1)S(1)}, u32[]{:S(2)}, u32[]{:S(2)}) async-start(bf16[4,64,2560]{2,1,0:T(8,128)(2,1)} %broadcast_in_dim.8), calls=%async_computation.2 | async-start | bytes 2621440 | tf_op jit(solution)/shard_map/all_to_all | solution.py:259
  69.3 0.1 slice.4
  69.4 0.1 reshape.28
  69.5 13.0 %all_gather.3.own_ref = bf16[128,2560]{1,0:T(8,128)(2,1)S(1)} all-gather(bf16[32,2560]{1,0:T(8,128)(2,1)S(1)} %reshape.28), channel_id=1, replica_groups=mesh['z'=16,'y'=4,'xl'=2,'xh'=2,'c'=2] {'xh','xl'}, dimensions={0}, use_global_device_ids=true | all-gather | bytes 819200 | tf_op jit(solution)/shard_map/all_gather | solution.py:263
  82.5 1.9 %collective-permute-start = (bf16[128,2560]{1,0:T(8,128)(2,1)S(1)}, bf16[128,2560]{1,0:T(8,128)(2,1)S(1)}, u32[]{:S(2)}, u32[]{:S(2)}) collective-permute-start(bf16[128,2560]{1,0:T(8,128)(2,1)S(1)} %all_gather.3.own_ref), channel_id=1, source_target_pairs={{0,1},{1,0},{2,3},{3,2},{4,5},{5,4},{6,7},{7,6},{8,9},{9,8},{10,11... | collective-permute-start | bytes 1966088 | tf_op jit(solution)/shard_map/ppermute | solution.py:264
  84.4 2.1 %collective-permute-done.other_ref = bf16[128,2560]{1,0:T(8,128)(2,1)S(1)} collective-permute-done((bf16[128,2560]{1,0:T(8,128)(2,1)S(1)}, bf16[128,2560]{1,0:T(8,128)(2,1)S(1)}, u32[]{:S(2)}, u32[]{:S(2)}) %collective-permute-start) | collective-permute-done | bytes 655392 | tf_op jit(solution)/shard_map/ppermute | solution.py:264
  86.5 0.0 all-to-all-done.2.cols_ref
  86.5 1.2 block_product.1
  87.7 34.0 %all_to_all.21.parts_ref = f32[128,4,128]{2,1,0:T(4,128)} all-to-all(f32[128,4,128]{2,1,0:T(4,128)S(1)} %block_product.1), channel_id=1, replica_groups=mesh['z'=16,'y'=4,'xl'=2,'xh'=2,'c'=2] {'z','xl','xh','c'}, dimensions={0} | all-to-all | bytes 524288 | tf_op jit(solution)/shard_map/all_to_all | solution.py:267
  121.6 2.0 %finish.1 = (f32[8,256]{1,0:T(8,128)}, f32[8,256]{1,0:T(8,128)}) custom-call(f32[128,4,128]{2,1,0:T(4,128)} %all_to_all.21.parts_ref, bf16[512,512]{1,0:T(8,128)(2,1)} %get-tuple-element.5.hot_ref), custom_call_target="tpu_custom_call" | custom-call | tf_op jit(solution)/shard_map/finish/pallas_call | solution.py:219
Async XLA Ops:
  9.2 9.0 %all-to-all-start = ((bf16[4,3,2,5120]{3,2,1,0:T(2,128)(2,1)}), bf16[4,3,2,5120]{3,2,1,0:T(2,128)(2,1)S(1)}, u32[]{:S(2)}, u32[]{:S(2)}) async-start(bf16[4,3,2,5120]{3,2,1,0:T(2,128)(2,1)} %pieces.1), calls=%async_computation | async-start | bytes 491520 | tf_op jit(solution)/shard_map/all_to_all | solution.py:253
  18.2 1.0 copy-start
  64.8 21.7 %all-to-all-start.2 = ((bf16[4,64,2560]{2,1,0:T(8,128)(2,1)}), bf16[4,64,2560]{2,1,0:T(8,128)(2,1)S(1)}, u32[]{:S(2)}, u32[]{:S(2)}) async-start(bf16[4,64,2560]{2,1,0:T(8,128)(2,1)} %broadcast_in_dim.8), calls=%async_computation.2 | async-start | bytes 2621440 | tf_op jit(solution)/shard_map/all_to_all | solution.py:259
  82.5 4.0 %collective-permute-start = (bf16[128,2560]{1,0:T(8,128)(2,1)S(1)}, bf16[128,2560]{1,0:T(8,128)(2,1)S(1)}, u32[]{:S(2)}, u32[]{:S(2)}) collective-permute-start(bf16[128,2560]{1,0:T(8,128)(2,1)S(1)} %all_gather.3.own_ref), channel_id=1, source_target_pairs={{0,1},{1,0},{2,3},{3,2},{4,5},{5,4},{6,7},{7,6},{8,9},{9,8},{10,11... | collective-permute-start | bytes 1966088 | tf_op jit(solution)/shard_map/ppermute | solution.py:264

commit v5 on v3

--- a/solution.py
+++ b/solution.py
@@ -20,7 +20,7 @@
 filter_radius = 4.5
 
 
-def filter_kernel(which, mixed_ref, rim_ref, out_ref, one, two, rim_term, pot):
+def filter_kernel(mixed_ref, rim_ref, out_ref, one, two, rim_term, pot):
     row = lax.broadcasted_iota(jnp.int32, (NZ, SPAN), 0)
     x = lax.rem(lax.broadcasted_iota(jnp.int32, (NZ, SPAN), 1), NX)
     zero = jnp.zeros((NZ, SPAN), jnp.float32)
@@ -40,7 +40,7 @@
         planes = [mixed_ref[s, orb] for s in range(4)]
         one[orb, :, PAD : PAD + PLANE] = jnp.concatenate(planes, axis=0).astype(jnp.float32)
         wrap(one, orb)
-        rim = rim_ref[which[0], orb].astype(jnp.float32)
+        rim = rim_ref[orb].astype(jnp.float32)
         low_far, low, high, high_far = (rim[k : k + 1] for k in range(4))
         rim_term[orb] = jnp.concatenate(
             [16.0 * low - low_far, -low, jnp.zeros((4, PLANE), jnp.float32), -high, 16.0 * high - high_far],
@@ -99,11 +99,11 @@
         last_body(chunk, 0)
 
 
-def filtered_and_applied(which, mixed, boundary):
+def filtered_and_applied(mixed, rim):
     whole = pl.BlockSpec(memory_space=pltpu.VMEM)
     return pl.pallas_call(
         filter_kernel,
-        in_specs=[pl.BlockSpec(memory_space=pltpu.SMEM), whole, whole],
+        in_specs=[whole, whole],
         out_specs=whole,
         out_shape=jax.ShapeDtypeStruct((4, NZ, PLANE), jnp.bfloat16),
         scratch_shapes=[
@@ -114,7 +114,7 @@
         ],
         compiler_params=pltpu.CompilerParams(vmem_limit_bytes=24 * 1024 * 1024),
         name="chebyshev_filter",
-    )(which, mixed, boundary)
+    )(mixed, rim)
 
 
 def swapped(values):
@@ -201,19 +201,51 @@
         in_specs=[whole],
         out_specs=[whole, whole],
         out_shape=[shape, shape],
+        compiler_params=pltpu.CompilerParams(vmem_limit_bytes=8 * 1024 * 1024),
         name="finish",
     )(parts)
 
 
+def pieces_kernel(which, orbitals_ref, potential_ref, rim_ref, out_ref, own_rim_ref, sems):
+    copies = [
+        pltpu.make_async_copy(orbitals_ref, out_ref.at[:, 0:2], sems.at[0]),
+        pltpu.make_async_copy(rim_ref.at[which[0]], own_rim_ref, sems.at[1]),
+    ]
+    for k in range(4):
+        copies.append(pltpu.make_async_copy(potential_ref, out_ref.at[k, 2], sems.at[2 + k]))
+    for copy in copies:
+        copy.start()
+    for copy in copies:
+        copy.wait()
+
+
+def pieces_of(which, orbitals, potential, boundary):
+    anywhere = pl.BlockSpec(memory_space=pl.ANY)
+    whole = pl.BlockSpec(memory_space=pltpu.VMEM)
+    return pl.pallas_call(
+        pieces_kernel,
+        in_specs=[pl.BlockSpec(memory_space=pltpu.SMEM), anywhere, anywhere, anywhere],
+        out_specs=[whole, whole],
+        out_shape=[
+            jax.ShapeDtypeStruct((4, 3, 2, PLANE), jnp.bfloat16),
+            jax.ShapeDtypeStruct((2, 4, PLANE), jnp.bfloat16),
+        ],
+        scratch_shapes=[pltpu.SemaphoreType.DMA((6,))],
+        compiler_params=pltpu.CompilerParams(vmem_limit_bytes=56 * 1024 * 1024),
+        name="pieces",
+    )(which, orbitals, potential, boundary)
+
+
 def per_device(orbitals, boundary, potential):
     own = lax.axis_index("xh") * 2 + lax.axis_index("c")
-    pieces = jnp.concatenate(
-        [orbitals.reshape(4, 2, 2, PLANE), jnp.broadcast_to(potential, (4, 1, 2, PLANE))], axis=1
+    pieces, own_rim = pieces_of(
+        own.astype(jnp.int32).reshape(1),
+        orbitals.reshape(4, 2, 2, PLANE),
+        potential,
+        boundary.reshape(4, 2, 4, PLANE),
     )
     mixed = lax.all_to_all(pieces, ("xh", "c"), split_axis=0, concat_axis=0, tiled=True)
-    fields = filtered_and_applied(
-        own.astype(jnp.int32).reshape(1), mixed, boundary.reshape(4, 2, 4, PLANE)
-    )
+    fields = filtered_and_applied(mixed, own_rim)
     shares = fields.reshape(4, SHARES, SHARE).transpose(1, 0, 2)
     shares = lax.all_to_all(shares, "z", split_axis=0, concat_axis=0, tiled=True)
     cols = shares.reshape(4 * SHARES, SHARE)

time: 114 us -> 113 us (level)
  blocking collectives: 83 us -> 91.8 us
  starting transfers between devices: 11.2 us -> 6.37 us
  waiting for transfers between devices: 6.27 us -> 2.07 us
  other arithmetic: 1.93 us -> 0 us
    all_to_all x0 -> x1, blocking collectives: none -> 9.01 us  [per_device(): lax.all_to_all(pieces, ('xh', 'c'), split_axis=0, concat_axis=0, tiled=True)]
    all_to_all x1 -> x0, starting transfers between devices: 4.8 us -> none  [per_device(): lax.all_to_all(pieces, ('xh', 'c'), split_axis=0, concat_axis=0, tiled=True)]
    all_to_all x1 -> x0, waiting for transfers between devices: 4.2 us -> none  [per_device(): lax.all_to_all(pieces, ('xh', 'c'), split_axis=0, concat_axis=0, tiled=True)]
    concatenate x1 -> x0, other arithmetic: 1.93 us -> none  [per_device(): jnp.concatenate([orbitals.reshape(4, 2, 2, PLANE), jnp.broadcast_to(poten...]
    pallas_call x1 -> x2, Pallas kernels: 4.24 us -> 5.96 us  [the longest x1 4.22 us: filtered_and_applied(): pl.pallas_call(filter_kernel, in_specs=[whole, whole], out_specs=whole, o...]
  transfers between devices with their start and end apart: 3 -> 2, of which waited for: 2 -> 1; matrix products, arithmetic and copies ran while one was open for 0% -> 0% of each run, Pallas kernels for 0% -> 0%
where the time goes in v5:
time: 113 us; the launch traced here: 112 us
  blocking collectives  91.8 us (81%)
  Pallas kernels  7.98 us (7%)
  starting transfers between devices  6.37 us (6%)
  local copies, waits for them, and re-layouts  2.69 us (2%)
  waiting for transfers between devices  2.07 us (2%)
    all_to_all x1, blocking collectives, per_device(): lax.all_to_all(shares, 'z', split_axis=0, concat_axis=0, tiled=True)  36 us
    all_to_all x1, blocking collectives, per_device(): lax.all_to_all(partial, ('z', 'xl', 'xh', 'c'), split_axis=0, concat_axis...  33.7 us
    all_gather x1, blocking collectives, per_device(): rows = lax.all_gather(rows, ('xh', 'xl'), axis=0, tiled=True)  13 us
    all_to_all x1, blocking collectives, per_device(): lax.all_to_all(pieces, ('xh', 'c'), split_axis=0, concat_axis=0, tiled=True)  9.01 us
    all_to_all x1, starting transfers between devices, per_device(): lax.all_to_all(jnp.broadcast_to(cols[None], (4, 4 * SHARES, SHARE)), 'y',...  4.46 us
    pallas_call x1, Pallas kernels, filtered_and_applied(): pl.pallas_call(filter_kernel, in_specs=[whole, whole], out_specs=whole, o...  4.22 us
  transfers between devices with their start and end apart: 2, of which 1 were waited for; matrix products, arithmetic and copies ran while one was open for 0% of the time, Pallas kernels for 0%

profile of v5, /device:TPU:6, one launch (start us, length us, event | category | flops | bytes accessed | tf_op | source)
XLA Modules:
  0.0 111.6 jit_solution(8881477193635303868)
XLA Ops:
  0.6 1.7 %pieces.1 = (bf16[4,3,2,5120]{3,2,1,0:T(2,128)(2,1)}, bf16[2,4,5120]{2,1,0:T(4,128)(2,1)}) custom-call(s32[1]{0:T(128)} %bitcast.1.which, bf16[4,2,2,5120]{3,2,1,0:T(2,128)(2,1)} %bitcast.9, bf16[2,5120]{1,0:T(2,128)(2,1)} %potential_ref.1, bf16[4,2,4,5120]{3,2,1,0:T(4,128)(2,1)} %bitcast.8), custom_call_target="tpu_custom_call" | custom-call | tf_op jit(solution)/shard_map/pieces/pallas_call | solution.py:225
  2.4 9.0 %all_to_all.20.mixed_ref = bf16[4,3,2,5120]{3,2,1,0:T(2,128)(2,1)S(1)} all-to-all(bf16[4,3,2,5120]{3,2,1,0:T(2,128)(2,1)} %get-tuple-element.4), channel_id=1, replica_groups=mesh['z'=16,'y'=4,'xl'=2,'xh'=2,'c'=2] {'xh','c'}, dimensions={0} | all-to-all | bytes 491520 | tf_op jit(solution)/shard_map/all_to_all | solution.py:247
  11.4 0.0 copy-start
  11.4 0.9 copy-done
  12.3 4.2 %chebyshev_filter.1 = bf16[4,8,5120]{2,1,0:T(8,128)(2,1)S(1)} custom-call(bf16[4,3,2,5120]{3,2,1,0:T(2,128)(2,1)S(1)} %all_to_all.20.mixed_ref, bf16[2,4,5120]{2,1,0:T(4,128)(2,1)S(1)} %copy-done), custom_call_target="tpu_custom_call" | custom-call | tf_op jit(solution)/shard_map/chebyshev_filter/pallas_call | solution.py:104
  16.5 0.1 reshape.27
  16.6 0.3 copy.7
  16.9 36.0 %all_to_all.21 = bf16[16,4,2560]{2,1,0:T(4,128)(2,1)S(1)} all-to-all(bf16[16,4,2560]{2,1,0:T(4,128)(2,1)S(1)} %bitcast.7), channel_id=1, replica_groups=mesh['z'=16,'y'=4,'xl'=2,'xh'=2,'c'=2] {'z'}, dimensions={0} | all-to-all | bytes 655360 | tf_op jit(solution)/shard_map/all_to_all | solution.py:250
  52.9 0.1 broadcast_in_dim.7
  52.9 1.2 %broadcast_in_dim.8 = bf16[4,64,2560]{2,1,0:T(8,128)(2,1)} broadcast(bf16[64,2560]{1,0:T(8,128)(2,1)S(1)} %broadcast_in_dim.7), dimensions={1,2} | broadcast | bytes 1638400 | tf_op jit(solution)/shard_map/broadcast_in_dim | solution.py:253
  54.1 4.5 %all-to-all-start.2 = ((bf16[4,64,2560]{2,1,0:T(8,128)(2,1)}), bf16[4,64,2560]{2,1,0:T(8,128)(2,1)S(1)}, u32[]{:S(2)}, u32[]{:S(2)}) async-start(bf16[4,64,2560]{2,1,0:T(8,128)(2,1)} %broadcast_in_dim.8), calls=%async_computation.2 | async-start | bytes 2621440 | tf_op jit(solution)/shard_map/all_to_all | solution.py:252
  58.6 0.1 slice.4
  58.7 0.1 reshape.28
  58.8 13.0 %all_gather.3.own_ref = bf16[128,2560]{1,0:T(8,128)(2,1)S(1)} all-gather(bf16[32,2560]{1,0:T(8,128)(2,1)S(1)} %reshape.28), channel_id=1, replica_groups=mesh['z'=16,'y'=4,'xl'=2,'xh'=2,'c'=2] {'xh','xl'}, dimensions={0}, use_global_device_ids=true | all-gather | bytes 819200 | tf_op jit(solution)/shard_map/all_gather | solution.py:256
  71.8 1.9 %collective-permute-start = (bf16[128,2560]{1,0:T(8,128)(2,1)S(1)}, bf16[128,2560]{1,0:T(8,128)(2,1)S(1)}, u32[]{:S(2)}, u32[]{:S(2)}) collective-permute-start(bf16[128,2560]{1,0:T(8,128)(2,1)S(1)} %all_gather.3.own_ref), channel_id=1, source_target_pairs={{0,1},{1,0},{2,3},{3,2},{4,5},{5,4},{6,7},{7,6},{8,9},{9,8},{10,11... | collective-permute-start | bytes 1966088 | tf_op jit(solution)/shard_map/ppermute | solution.py:257
  73.7 2.1 %collective-permute-done.other_ref = bf16[128,2560]{1,0:T(8,128)(2,1)S(1)} collective-permute-done((bf16[128,2560]{1,0:T(8,128)(2,1)S(1)}, bf16[128,2560]{1,0:T(8,128)(2,1)S(1)}, u32[]{:S(2)}, u32[]{:S(2)}) %collective-permute-start) | collective-permute-done | bytes 655392 | tf_op jit(solution)/shard_map/ppermute | solution.py:257
  75.8 0.0 all-to-all-done.2.cols_ref
  75.8 1.2 %block_product.1 = f32[128,4,128]{2,1,0:T(4,128)S(1)} custom-call(s32[1]{0:T(128)} %bitcast.core_ref, bf16[128,2560]{1,0:T(8,128)(2,1)S(1)} %all_gather.3.own_ref, bf16[128,2560]{1,0:T(8,128)(2,1)S(1)} %collective-permute-done.other_ref, bf16[4,64,2560]{2,1,0:T(8,128)(2,1)S(1)} %all-to-all-done.2.cols_ref), custom_call_target="tpu_custom_call" | custom-call | tf_op jit(solution)/shard_map/block_product/pallas_call | solution.py:150
  77.0 33.7 %all_to_all.22.parts_ref = f32[128,4,128]{2,1,0:T(4,128)S(1)} all-to-all(f32[128,4,128]{2,1,0:T(4,128)S(1)} %block_product.1), channel_id=1, replica_groups=mesh['z'=16,'y'=4,'xl'=2,'xh'=2,'c'=2] {'z','xl','xh','c'}, dimensions={0} | all-to-all | bytes 524288 | tf_op jit(solution)/shard_map/all_to_all | solution.py:260
  110.7 0.9 finish.1
Async XLA Ops:
  11.4 0.9 copy-start
  54.1 21.7 %all-to-all-start.2 = ((bf16[4,64,2560]{2,1,0:T(8,128)(2,1)}), bf16[4,64,2560]{2,1,0:T(8,128)(2,1)S(1)}, u32[]{:S(2)}, u32[]{:S(2)}) async-start(bf16[4,64,2560]{2,1,0:T(8,128)(2,1)} %broadcast_in_dim.8), calls=%async_computation.2 | async-start | bytes 2621440 | tf_op jit(solution)/shard_map/all_to_all | solution.py:252
  71.8 4.0 %collective-permute-start = (bf16[128,2560]{1,0:T(8,128)(2,1)S(1)}, bf16[128,2560]{1,0:T(8,128)(2,1)S(1)}, u32[]{:S(2)}, u32[]{:S(2)}) collective-permute-start(bf16[128,2560]{1,0:T(8,128)(2,1)S(1)} %all_gather.3.own_ref), channel_id=1, source_target_pairs={{0,1},{1,0},{2,3},{3,2},{4,5},{5,4},{6,7},{7,6},{8,9},{9,8},{10,11... | collective-permute-start | bytes 1966088 | tf_op jit(solution)/shard_map/ppermute | solution.py:257

commit v6 on v5

--- a/solution.py
+++ b/solution.py
@@ -21,13 +21,11 @@
 
 
 def filter_kernel(mixed_ref, rim_ref, out_ref, one, two, rim_term, pot):
-    row = lax.broadcasted_iota(jnp.int32, (NZ, SPAN), 0)
     x = lax.rem(lax.broadcasted_iota(jnp.int32, (NZ, SPAN), 1), NX)
-    zero = jnp.zeros((NZ, SPAN), jnp.float32)
-    below_1 = jnp.where(row >= 1, zero + 16.0, zero)
-    above_1 = jnp.where(row <= NZ - 2, zero + 16.0, zero)
-    below_2 = jnp.where(row >= 2, zero + 1.0, zero)
-    above_2 = jnp.where(row <= NZ - 3, zero + 1.0, zero)
+    row, col = (lax.broadcasted_iota(jnp.int32, (2 * NZ, 2 * NZ), k) for k in range(2))
+    apart = jnp.where((row >= NZ) == (col >= NZ), jnp.abs(row - col), 3)
+    weight = jnp.where(apart == 0, -90.0, jnp.where(apart == 1, 16.0, jnp.where(apart == 2, -1.0, 0.0)))
+    z_matrix = weight.astype(jnp.bfloat16)
     first, last = x == 0, x == NX - 1
     first_two, last_two = x <= 1, x >= NX - 2
 
@@ -47,7 +45,11 @@
             axis=0,
         )
 
-    def apply_ham(ref, orb, at):
+    def z_parts(ref, at):
+        both = jnp.concatenate([ref[orb, :, pl.ds(at + PAD, SPAN)] for orb in range(2)], axis=0)
+        return jnp.dot(z_matrix, both.astype(jnp.bfloat16), preferred_element_type=jnp.float32)
+
+    def apply_ham(ref, orb, at, z_part):
         window = ref[orb, :, pl.ds(at, SPAN + 2 * PAD)]
         width = SPAN + 2 * PAD
 
@@ -61,9 +63,7 @@
             last_two, cells(2 - NX), cells(2)
         )
         far = far + (cells(2 * NX) + cells(-2 * NX))
-        z_near = below_1 * pltpu.roll(middle, 1, 0) + above_1 * pltpu.roll(middle, NZ - 1, 0)
-        z_far = below_2 * pltpu.roll(middle, 2, 0) + above_2 * pltpu.roll(middle, NZ - 2, 0)
-        total = (16.0 * near - far) + (z_near - z_far) - 90.0 * middle
+        total = (16.0 * near - far) + z_part[NZ * orb : NZ * orb + NZ]
         total = total + rim_term[orb, :, pl.ds(at, SPAN)]
         return total * (-0.5 / 12.0) + pot[:, pl.ds(at, SPAN)] * middle, middle
 
@@ -72,8 +72,9 @@
 
         def body(chunk, carry, step=step, current=current, earlier=earlier):
             at = chunk * SPAN
+            z_part = z_parts(current, at)
             for orb in range(2):
-                with_h, middle = apply_ham(current, orb, at)
+                with_h, middle = apply_ham(current, orb, at, z_part)
                 following = (with_h - filter_center * middle) * (1.0 / filter_radius)
                 place = (orb, slice(None), pl.ds(at + PAD, SPAN))
                 if step > 0:
@@ -89,8 +90,9 @@
 
     def last_body(chunk, carry):
         at = chunk * SPAN
+        z_part = z_parts(current, at)
         for orb in range(2):
-            with_h, middle = apply_ham(current, orb, at)
+            with_h, middle = apply_ham(current, orb, at, z_part)
             out_ref[orb, :, pl.ds(at, SPAN)] = middle.astype(jnp.bfloat16)
             out_ref[2 + orb, :, pl.ds(at, SPAN)] = with_h.astype(jnp.bfloat16)
         return carry
@@ -206,46 +208,35 @@
     )(parts)
 
 
-def pieces_kernel(which, orbitals_ref, potential_ref, rim_ref, out_ref, own_rim_ref, sems):
-    copies = [
-        pltpu.make_async_copy(orbitals_ref, out_ref.at[:, 0:2], sems.at[0]),
-        pltpu.make_async_copy(rim_ref.at[which[0]], own_rim_ref, sems.at[1]),
-    ]
+def pieces_kernel(orbitals_ref, potential_ref, out_ref, sems):
+    copies = [pltpu.make_async_copy(orbitals_ref, out_ref.at[:, 0:2], sems.at[0])]
     for k in range(4):
-        copies.append(pltpu.make_async_copy(potential_ref, out_ref.at[k, 2], sems.at[2 + k]))
+        copies.append(pltpu.make_async_copy(potential_ref, out_ref.at[k, 2], sems.at[1 + k]))
     for copy in copies:
         copy.start()
     for copy in copies:
         copy.wait()
 
 
-def pieces_of(which, orbitals, potential, boundary):
+def pieces_of(orbitals, potential):
     anywhere = pl.BlockSpec(memory_space=pl.ANY)
-    whole = pl.BlockSpec(memory_space=pltpu.VMEM)
     return pl.pallas_call(
         pieces_kernel,
-        in_specs=[pl.BlockSpec(memory_space=pltpu.SMEM), anywhere, anywhere, anywhere],
-        out_specs=[whole, whole],
-        out_shape=[
-            jax.ShapeDtypeStruct((4, 3, 2, PLANE), jnp.bfloat16),
-            jax.ShapeDtypeStruct((2, 4, PLANE), jnp.bfloat16),
-        ],
-        scratch_shapes=[pltpu.SemaphoreType.DMA((6,))],
+        in_specs=[anywhere, anywhere],
+        out_specs=pl.BlockSpec(memory_space=pltpu.VMEM),
+        out_shape=jax.ShapeDtypeStruct((4, 3, 2, PLANE), jnp.bfloat16),
+        scratch_shapes=[pltpu.SemaphoreType.DMA((5,))],
         compiler_params=pltpu.CompilerParams(vmem_limit_bytes=56 * 1024 * 1024),
         name="pieces",
-    )(which, orbitals, potential, boundary)
+    )(orbitals, potential)
 
 
 def per_device(orbitals, boundary, potential):
     own = lax.axis_index("xh") * 2 + lax.axis_index("c")
-    pieces, own_rim = pieces_of(
-        own.astype(jnp.int32).reshape(1),
-        orbitals.reshape(4, 2, 2, PLANE),
-        potential,
-        boundary.reshape(4, 2, 4, PLANE),
-    )
+    pieces = pieces_of(orbitals.reshape(4, 2, 2, PLANE), potential)
     mixed = lax.all_to_all(pieces, ("xh", "c"), split_axis=0, concat_axis=0, tiled=True)
-    fields = filtered_and_applied(mixed, own_rim)
+    rim = lax.dynamic_index_in_dim(boundary.reshape(4, 2, 4, PLANE), own, 0, keepdims=False)
+    fields = filtered_and_applied(mixed, rim)
     shares = fields.reshape(4, SHARES, SHARE).transpose(1, 0, 2)
     shares = lax.all_to_all(shares, "z", split_axis=0, concat_axis=0, tiled=True)
     cols = shares.reshape(4 * SHARES, SHARE)

time: 113 us -> 111 us (0.982)
  blocking collectives: 91.8 us -> 82.9 us
  starting transfers between devices: 6.37 us -> 11.2 us
  waiting for transfers between devices: 2.07 us -> 6.23 us
    all_to_all x1 -> x0, blocking collectives: 9.01 us -> none  [per_device(): lax.all_to_all(pieces, ('xh', 'c'), split_axis=0, concat_axis=0, tiled=True)]
    all_to_all x0 -> x1, starting transfers between devices: none -> 4.81 us  [per_device(): lax.all_to_all(pieces, ('xh', 'c'), split_axis=0, concat_axis=0, tiled=True)]
    all_to_all x0 -> x1, waiting for transfers between devices: none -> 4.16 us  [per_device(): lax.all_to_all(pieces, ('xh', 'c'), split_axis=0, concat_axis=0, tiled=True)]
  transfers between devices with their start and end apart: 2 -> 3, of which waited for: 1 -> 2; matrix products, arithmetic and copies ran while one was open for 0% -> 0% of each run, Pallas kernels for 0% -> 0%
where the time goes in v6:
time: 111 us; the launch traced here: 110 us
  blocking collectives  82.9 us (75%)
  starting transfers between devices  11.2 us (10%)
  Pallas kernels  7.32 us (7%)
  waiting for transfers between devices  6.23 us (6%)
  local copies, waits for them, and re-layouts  1.83 us (2%)
    all_to_all x1, blocking collectives, per_device(): lax.all_to_all(shares, 'z', split_axis=0, concat_axis=0, tiled=True)  36 us
    all_to_all x1, blocking collectives, per_device(): lax.all_to_all(partial, ('z', 'xl', 'xh', 'c'), split_axis=0, concat_axis...  33.9 us
    all_gather x1, blocking collectives, per_device(): rows = lax.all_gather(rows, ('xh', 'xl'), axis=0, tiled=True)  13 us
    all_to_all x1, starting transfers between devices, per_device(): lax.all_to_all(pieces, ('xh', 'c'), split_axis=0, concat_axis=0, tiled=True)  4.81 us
    all_to_all x1, starting transfers between devices, per_device(): lax.all_to_all(jnp.broadcast_to(cols[None], (4, 4 * SHARES, SHARE)), 'y',...  4.46 us
    all_to_all x1, waiting for transfers between devices, per_device(): lax.all_to_all(pieces, ('xh', 'c'), split_axis=0, concat_axis=0, tiled=True)  4.16 us
    pallas_call x1, Pallas kernels, filtered_and_applied(): pl.pallas_call(filter_kernel, in_specs=[whole, whole], out_specs=whole, o...  3.6 us
  transfers between devices with their start and end apart: 3, of which 2 were waited for; matrix products, arithmetic and copies ran while one was open for 0% of the time, Pallas kernels for 0%

profile of v6, /device:TPU:6, one launch (start us, length us, event | category | flops | bytes accessed | tf_op | source)
XLA Modules:
  0.0 110.2 jit_solution(14400533489134838285)
XLA Ops:
  0.6 0.0 copy-start
  0.6 1.7 %pieces.1 = bf16[4,3,2,5120]{3,2,1,0:T(2,128)(2,1)} custom-call(bf16[4,2,2,5120]{3,2,1,0:T(2,128)(2,1)} %bitcast.10, bf16[2,5120]{1,0:T(2,128)(2,1)} %potential_ref.1), custom_call_target="tpu_custom_call" | custom-call | tf_op jit(solution)/shard_map/pieces/pallas_call | solution.py:223
  2.4 4.8 %all-to-all-start = ((bf16[4,3,2,5120]{3,2,1,0:T(2,128)(2,1)}), bf16[4,3,2,5120]{3,2,1,0:T(2,128)(2,1)S(1)}, u32[]{:S(2)}, u32[]{:S(2)}) async-start(bf16[4,3,2,5120]{3,2,1,0:T(2,128)(2,1)} %pieces.1), calls=%async_computation | async-start | bytes 491520 | tf_op jit(solution)/shard_map/all_to_all | solution.py:237
  7.2 0.0 copy-done
  7.2 4.2 %all-to-all-done.mixed_ref = bf16[4,3,2,5120]{3,2,1,0:T(2,128)(2,1)S(1)} async-done(((bf16[4,3,2,5120]{3,2,1,0:T(2,128)(2,1)}), bf16[4,3,2,5120]{3,2,1,0:T(2,128)(2,1)S(1)}, u32[]{:S(2)}, u32[]{:S(2)}) %all-to-all-start) | async-done | bytes 245792 | tf_op jit(solution)/shard_map/all_to_all | solution.py:237
  11.4 3.6 %chebyshev_filter.1 = bf16[4,8,5120]{2,1,0:T(8,128)(2,1)S(1)} custom-call(bf16[4,3,2,5120]{3,2,1,0:T(2,128)(2,1)S(1)} %all-to-all-done.mixed_ref, bf16[2,4,5120]{2,1,0:T(4,128)(2,1)S(1)} %dynamic-slice_bitcast_fusion.rim_ref), custom_call_target="tpu_custom_call" | custom-call | tf_op jit(solution)/shard_map/chebyshev_filter/pallas_call | solution.py:106
  15.0 0.1 reshape.23
  15.1 0.3 copy.7
  15.4 36.0 %all_to_all.20 = bf16[16,4,2560]{2,1,0:T(4,128)(2,1)S(1)} all-to-all(bf16[16,4,2560]{2,1,0:T(4,128)(2,1)S(1)} %bitcast.9), channel_id=1, replica_groups=mesh['z'=16,'y'=4,'xl'=2,'xh'=2,'c'=2] {'z'}, dimensions={0} | all-to-all | bytes 655360 | tf_op jit(solution)/shard_map/all_to_all | solution.py:241
  51.3 0.1 broadcast_in_dim.7
  51.4 1.2 %broadcast_in_dim.8 = bf16[4,64,2560]{2,1,0:T(8,128)(2,1)} broadcast(bf16[64,2560]{1,0:T(8,128)(2,1)S(1)} %broadcast_in_dim.7), dimensions={1,2} | broadcast | bytes 1638400 | tf_op jit(solution)/shard_map/broadcast_in_dim | solution.py:244
  52.6 4.5 %all-to-all-start.2 = ((bf16[4,64,2560]{2,1,0:T(8,128)(2,1)}), bf16[4,64,2560]{2,1,0:T(8,128)(2,1)S(1)}, u32[]{:S(2)}, u32[]{:S(2)}) async-start(bf16[4,64,2560]{2,1,0:T(8,128)(2,1)} %broadcast_in_dim.8), calls=%async_computation.2 | async-start | bytes 2621440 | tf_op jit(solution)/shard_map/all_to_all | solution.py:243
  57.0 0.1 slice.4
  57.2 0.1 reshape.24
  57.2 13.0 %all_gather.3.own_ref = bf16[128,2560]{1,0:T(8,128)(2,1)S(1)} all-gather(bf16[32,2560]{1,0:T(8,128)(2,1)S(1)} %reshape.24), channel_id=1, replica_groups=mesh['z'=16,'y'=4,'xl'=2,'xh'=2,'c'=2] {'xh','xl'}, dimensions={0}, use_global_device_ids=true | all-gather | bytes 819200 | tf_op jit(solution)/shard_map/all_gather | solution.py:247
  70.3 1.9 %collective-permute-start = (bf16[128,2560]{1,0:T(8,128)(2,1)S(1)}, bf16[128,2560]{1,0:T(8,128)(2,1)S(1)}, u32[]{:S(2)}, u32[]{:S(2)}) collective-permute-start(bf16[128,2560]{1,0:T(8,128)(2,1)S(1)} %all_gather.3.own_ref), channel_id=1, source_target_pairs={{0,1},{1,0},{2,3},{3,2},{4,5},{5,4},{6,7},{7,6},{8,9},{9,8},{10,11... | collective-permute-start | bytes 1966088 | tf_op jit(solution)/shard_map/ppermute | solution.py:248
  72.2 2.1 %collective-permute-done.other_ref = bf16[128,2560]{1,0:T(8,128)(2,1)S(1)} collective-permute-done((bf16[128,2560]{1,0:T(8,128)(2,1)S(1)}, bf16[128,2560]{1,0:T(8,128)(2,1)S(1)}, u32[]{:S(2)}, u32[]{:S(2)}) %collective-permute-start) | collective-permute-done | bytes 655392 | tf_op jit(solution)/shard_map/ppermute | solution.py:248
  74.3 0.0 all-to-all-done.2.cols_ref
  74.3 1.1 %block_product.1 = f32[128,4,128]{2,1,0:T(4,128)S(1)} custom-call(s32[1]{0:T(128)} %bitcast.core_ref, bf16[128,2560]{1,0:T(8,128)(2,1)S(1)} %all_gather.3.own_ref, bf16[128,2560]{1,0:T(8,128)(2,1)S(1)} %collective-permute-done.other_ref, bf16[4,64,2560]{2,1,0:T(8,128)(2,1)S(1)} %all-to-all-done.2.cols_ref), custom_call_target="tpu_custom_call" | custom-call | tf_op jit(solution)/shard_map/block_product/pallas_call | solution.py:152
  75.4 33.9 %all_to_all.21.parts_ref = f32[128,4,128]{2,1,0:T(4,128)S(1)} all-to-all(f32[128,4,128]{2,1,0:T(4,128)S(1)} %block_product.1), channel_id=1, replica_groups=mesh['z'=16,'y'=4,'xl'=2,'xh'=2,'c'=2] {'z','xl','xh','c'}, dimensions={0} | all-to-all | bytes 524288 | tf_op jit(solution)/shard_map/all_to_all | solution.py:251
  109.3 0.9 finish.1
  (1 shorter events, 0.0 us)
Async XLA Ops:
  0.6 6.5 %copy-start = (bf16[8,4,5120]{2,1,0:T(4,128)(2,1)S(1)}, bf16[8,4,5120]{2,1,0:T(4,128)(2,1)}, u32[]{:S(2)}) copy-start(bf16[8,4,5120]{2,1,0:T(4,128)(2,1)} %param.4) | copy-start | bytes 983044
  2.4 9.0 %all-to-all-start = ((bf16[4,3,2,5120]{3,2,1,0:T(2,128)(2,1)}), bf16[4,3,2,5120]{3,2,1,0:T(2,128)(2,1)S(1)}, u32[]{:S(2)}, u32[]{:S(2)}) async-start(bf16[4,3,2,5120]{3,2,1,0:T(2,128)(2,1)} %pieces.1), calls=%async_computation | async-start | bytes 491520 | tf_op jit(solution)/shard_map/all_to_all | solution.py:237
  52.6 21.7 %all-to-all-start.2 = ((bf16[4,64,2560]{2,1,0:T(8,128)(2,1)}), bf16[4,64,2560]{2,1,0:T(8,128)(2,1)S(1)}, u32[]{:S(2)}, u32[]{:S(2)}) async-start(bf16[4,64,2560]{2,1,0:T(8,128)(2,1)} %broadcast_in_dim.8), calls=%async_computation.2 | async-start | bytes 2621440 | tf_op jit(solution)/shard_map/all_to_all | solution.py:243
  70.3 4.0 %collective-permute-start = (bf16[128,2560]{1,0:T(8,128)(2,1)S(1)}, bf16[128,2560]{1,0:T(8,128)(2,1)S(1)}, u32[]{:S(2)}, u32[]{:S(2)}) collective-permute-start(bf16[128,2560]{1,0:T(8,128)(2,1)S(1)} %all_gather.3.own_ref), channel_id=1, source_target_pairs={{0,1},{1,0},{2,3},{3,2},{4,5},{5,4},{6,7},{7,6},{8,9},{9,8},{10,11... | collective-permute-start | bytes 1966088 | tf_op jit(solution)/shard_map/ppermute | solution.py:248

commit v7 on v6

--- a/solution.py
+++ b/solution.py
@@ -160,7 +160,30 @@
     )(core, own, other, cols)
 
 
-def finish_kernel(parts_ref, correlation_ref, projected_ref):
+def places_kernel(hot_ref):
+    at = lax.broadcasted_iota(jnp.int32, (1, 512), 1)
+
+    def field(shift, count):
+        return lax.shift_right_logical(at, shift) & (count - 1)
+
+    group = field(3, 2) * 4 + field(1, 4)
+    source = group * 64 + field(4, 4) * 16 + field(6, 4) * 4 + field(8, 2) * 2 + field(0, 2)
+    hot = jnp.where(lax.broadcasted_iota(jnp.int32, (512, 512), 0) == source, 1.0, 0.0)
+    hot_ref[...] = hot.astype(jnp.bfloat16)
+
+
+def places():
+    return pl.pallas_call(
+        places_kernel,
+        out_specs=pl.BlockSpec(memory_space=pltpu.VMEM),
+        out_shape=jax.ShapeDtypeStruct((512, 512), jnp.bfloat16),
+        compiler_params=pltpu.CompilerParams(vmem_limit_bytes=8 * 1024 * 1024),
+        cost_estimate=pl.CostEstimate(flops=1000000, bytes_accessed=524288, transcendentals=0),
+        name="places",
+    )()
+
+
+def finish_kernel(parts_ref, hot_ref, correlation_ref, projected_ref):
     left = lax.broadcasted_iota(jnp.int32, (4, 128), 1) < 64
     pieces = []
     for pair in range(4):
@@ -172,14 +195,6 @@
         high = jnp.where(left, swapped(one), two)
         pieces.append(jnp.concatenate([low, high], axis=0))
     given = jnp.concatenate(pieces, axis=1) * (1.0 / (NZ * PLANE))
-    at = lax.broadcasted_iota(jnp.int32, (1, 512), 1)
-
-    def field(shift, count):
-        return lax.shift_right_logical(at, shift) & (count - 1)
-
-    group = field(3, 2) * 4 + field(1, 4)
-    source = group * 64 + field(4, 4) * 16 + field(6, 4) * 4 + field(8, 2) * 2 + field(0, 2)
-    hot = jnp.where(lax.broadcasted_iota(jnp.int32, (512, 512), 0) == source, 1.0, 0.0)
     top = given.astype(jnp.bfloat16)
     rest = given - top.astype(jnp.float32)
     middle = rest.astype(jnp.bfloat16)
@@ -188,24 +203,24 @@
         [top.astype(jnp.float32), middle.astype(jnp.float32), last.astype(jnp.float32)], axis=0
     )
     placed = jnp.dot(
-        split.astype(jnp.bfloat16), hot.astype(jnp.bfloat16), preferred_element_type=jnp.float32
+        split.astype(jnp.bfloat16), hot_ref[...], preferred_element_type=jnp.float32
     )
     placed = (placed[16:] + placed[8:16]) + placed[:8]
     correlation_ref[...] = placed[:, :256]
     projected_ref[...] = placed[:, 256:]
 
 
-def finish(parts):
+def finish(parts, hot):
     shape = jax.ShapeDtypeStruct((8, 256), jnp.float32)
     whole = pl.BlockSpec(memory_space=pltpu.VMEM)
     return pl.pallas_call(
         finish_kernel,
-        in_specs=[whole],
+        in_specs=[whole, whole],
         out_specs=[whole, whole],
         out_shape=[shape, shape],
         compiler_params=pltpu.CompilerParams(vmem_limit_bytes=8 * 1024 * 1024),
         name="finish",
-    )(parts)
+    )(parts, hot)
 
 
 def pieces_kernel(orbitals_ref, potential_ref, out_ref, sems):
@@ -231,25 +246,44 @@
     )(orbitals, potential)
 
 
+def spread_kernel(values_ref, out_ref, sems):
+    copies = [pltpu.make_async_copy(values_ref, out_ref.at[k], sems.at[k]) for k in range(4)]
+    for copy in copies:
+        copy.start()
+    for copy in copies:
+        copy.wait()
+
+
+def spread(values):
+    return pl.pallas_call(
+        spread_kernel,
+        in_specs=[pl.BlockSpec(memory_space=pltpu.VMEM)],
+        out_specs=pl.BlockSpec(memory_space=pl.ANY),
+        out_shape=jax.ShapeDtypeStruct((4,) + values.shape, values.dtype),
+        scratch_shapes=[pltpu.SemaphoreType.DMA((4,))],
+        compiler_params=pltpu.CompilerParams(vmem_limit_bytes=4 * 1024 * 1024),
+        name="spread",
+    )(values)
+
+
 def per_device(orbitals, boundary, potential):
     own = lax.axis_index("xh") * 2 + lax.axis_index("c")
     pieces = pieces_of(orbitals.reshape(4, 2, 2, PLANE), potential)
     mixed = lax.all_to_all(pieces, ("xh", "c"), split_axis=0, concat_axis=0, tiled=True)
+    hot = places()
     rim = lax.dynamic_index_in_dim(boundary.reshape(4, 2, 4, PLANE), own, 0, keepdims=False)
     fields = filtered_and_applied(mixed, rim)
     shares = fields.reshape(4, SHARES, SHARE).transpose(1, 0, 2)
     shares = lax.all_to_all(shares, "z", split_axis=0, concat_axis=0, tiled=True)
     cols = shares.reshape(4 * SHARES, SHARE)
-    cols = lax.all_to_all(
-        jnp.broadcast_to(cols[None], (4, 4 * SHARES, SHARE)), "y", split_axis=0, concat_axis=0, tiled=True
-    )
+    cols = lax.all_to_all(spread(cols), "y", split_axis=0, concat_axis=0, tiled=True)
     rows = shares[:, :2].reshape(2 * SHARES, SHARE)
     rows = lax.all_gather(rows, ("xh", "xl"), axis=0, tiled=True)
     other = lax.ppermute(rows, "c", [(0, 1), (1, 0)])
     core = lax.axis_index("c").astype(jnp.int32).reshape(1)
     partial = block_product(core, rows, other, cols)
     parts = lax.all_to_all(partial, ("z", "xl", "xh", "c"), split_axis=0, concat_axis=0, tiled=True)
-    return tuple(finish(parts))
+    return tuple(finish(parts, hot))
 
 
 def solution(mesh):

time: 111 us -> 112 us (level)
  blocking collectives: 82.9 us -> 49 us
  waiting for transfers between devices: 6.23 us -> 28.3 us
  starting transfers between devices: 11.2 us -> 23.1 us
  Pallas kernels: 7.32 us -> 9.25 us
  local copies, waits for them, and re-layouts: 1.83 us -> 0.67 us
    all_to_all x1 -> x0, blocking collectives: 33.9 us -> none  [per_device(): lax.all_to_all(partial, ('z', 'xl', 'xh', 'c'), split_axis=0, concat_axis...]
    all_to_all x1 -> x2, waiting for transfers between devices: 0.01 us -> 22.1 us  [the longest x1 22.1 us: per_device(): lax.all_to_all(partial, ('z', 'xl', 'xh', 'c'), split_axis=0, concat_axis...]
    all_to_all x1 -> x2, starting transfers between devices: 4.46 us -> 16.4 us  [the longest x1 11.9 us: per_device(): lax.all_to_all(partial, ('z', 'xl', 'xh', 'c'), split_axis=0, concat_axis...]
    broadcast_in_dim x2 -> x0, local copies, waits for them, and re-layouts: 1.24 us -> none  [per_device(): jnp.broadcast_to(cols[None], (4, 4 * SHARES, SHARE))]
    pallas_call x1 -> x3, Pallas kernels: 0.87 us -> 2.08 us  [the longest x1 1.11 us: spread(): pl.pallas_call(spread_kernel, in_specs=[pl.BlockSpec(memory_space=pltpu.V...]
  transfers between devices with their start and end apart: 3 -> 4, of which waited for: 2 -> 3; matrix products, arithmetic and copies ran while one was open for 0% -> 0% of each run, Pallas kernels for 0% -> 0%
where the time goes in v7:
time: 112 us; the launch traced here: 111 us
  blocking collectives  49 us (44%)
  waiting for transfers between devices  28.3 us (25%)
  starting transfers between devices  23.1 us (21%)
  Pallas kernels  9.25 us (8%)
    all_to_all x1, blocking collectives, per_device(): lax.all_to_all(shares, 'z', split_axis=0, concat_axis=0, tiled=True)  36 us
    all_to_all x1, waiting for transfers between devices, per_device(): lax.all_to_all(partial, ('z', 'xl', 'xh', 'c'), split_axis=0, concat_axis...  22.1 us
    all_gather x1, blocking collectives, per_device(): rows = lax.all_gather(rows, ('xh', 'xl'), axis=0, tiled=True)  13 us
    all_to_all x1, starting transfers between devices, per_device(): lax.all_to_all(partial, ('z', 'xl', 'xh', 'c'), split_axis=0, concat_axis...  11.9 us
    all_to_all x1, starting transfers between devices, per_device(): lax.all_to_all(pieces, ('xh', 'c'), split_axis=0, concat_axis=0, tiled=True)  4.81 us
    all_to_all x1, starting transfers between devices, per_device(): lax.all_to_all(spread(cols), 'y', split_axis=0, concat_axis=0, tiled=True)  4.48 us
    all_to_all x1, waiting for transfers between devices, per_device(): lax.all_to_all(pieces, ('xh', 'c'), split_axis=0, concat_axis=0, tiled=True)  4.16 us
    pallas_call x1, Pallas kernels, filtered_and_applied(): pl.pallas_call(filter_kernel, in_specs=[whole, whole], out_specs=whole, o...  3.6 us
  transfers between devices with their start and end apart: 4, of which 3 were waited for; matrix products, arithmetic and copies ran while one was open for 0% of the time, Pallas kernels for 0%

profile of v7, /device:TPU:6, one launch (start us, length us, event | category | flops | bytes accessed | tf_op | source)
XLA Modules:
  0.0 111.0 jit_solution(6271994179400042383)
XLA Ops:
  0.6 0.0 copy-start
  0.6 1.7 %pieces.1 = bf16[4,3,2,5120]{3,2,1,0:T(2,128)(2,1)} custom-call(bf16[4,2,2,5120]{3,2,1,0:T(2,128)(2,1)} %bitcast.10, bf16[2,5120]{1,0:T(2,128)(2,1)} %potential_ref.1), custom_call_target="tpu_custom_call" | custom-call | tf_op jit(solution)/shard_map/pieces/pallas_call | solution.py:238
  2.4 4.8 %all-to-all-start = ((bf16[4,3,2,5120]{3,2,1,0:T(2,128)(2,1)}), bf16[4,3,2,5120]{3,2,1,0:T(2,128)(2,1)S(1)}, u32[]{:S(2)}, u32[]{:S(2)}) async-start(bf16[4,3,2,5120]{3,2,1,0:T(2,128)(2,1)} %pieces.1), calls=%async_computation | async-start | bytes 491520 | tf_op jit(solution)/shard_map/all_to_all | solution.py:272
  7.2 0.0 copy-done
  7.2 4.2 %all-to-all-done.mixed_ref = bf16[4,3,2,5120]{3,2,1,0:T(2,128)(2,1)S(1)} async-done(((bf16[4,3,2,5120]{3,2,1,0:T(2,128)(2,1)}), bf16[4,3,2,5120]{3,2,1,0:T(2,128)(2,1)S(1)}, u32[]{:S(2)}, u32[]{:S(2)}) %all-to-all-start) | async-done | bytes 245792 | tf_op jit(solution)/shard_map/all_to_all | solution.py:272
  11.4 3.6 %chebyshev_filter.1 = bf16[4,8,5120]{2,1,0:T(8,128)(2,1)S(1)} custom-call(bf16[4,3,2,5120]{3,2,1,0:T(2,128)(2,1)S(1)} %all-to-all-done.mixed_ref, bf16[2,4,5120]{2,1,0:T(4,128)(2,1)S(1)} %dynamic-slice_bitcast_fusion.rim_ref), custom_call_target="tpu_custom_call" | custom-call | tf_op jit(solution)/shard_map/chebyshev_filter/pallas_call | solution.py:106
  15.0 0.1 reshape.25
  15.1 0.3 copy.7
  15.4 36.0 %all_to_all.20 = bf16[16,4,2560]{2,1,0:T(4,128)(2,1)S(1)} all-to-all(bf16[16,4,2560]{2,1,0:T(4,128)(2,1)S(1)} %bitcast.9), channel_id=1, replica_groups=mesh['z'=16,'y'=4,'xl'=2,'xh'=2,'c'=2] {'z'}, dimensions={0} | all-to-all | bytes 655360 | tf_op jit(solution)/shard_map/all_to_all | solution.py:277
  51.3 0.1 reshape.27.values_ref
  51.4 1.1 spread.1
  52.5 4.5 %all-to-all-start.2 = ((bf16[4,64,2560]{2,1,0:T(8,128)(2,1)}), bf16[4,64,2560]{2,1,0:T(8,128)(2,1)S(1)}, u32[]{:S(2)}, u32[]{:S(2)}) async-start(bf16[4,64,2560]{2,1,0:T(8,128)(2,1)} %spread.1), calls=%async_computation.2 | async-start | bytes 2621440 | tf_op jit(solution)/shard_map/all_to_all | solution.py:279
  57.0 0.1 slice.4
  57.1 0.1 reshape.26
  57.2 13.0 %all_gather.3.own_ref = bf16[128,2560]{1,0:T(8,128)(2,1)S(1)} all-gather(bf16[32,2560]{1,0:T(8,128)(2,1)S(1)} %reshape.26), channel_id=1, replica_groups=mesh['z'=16,'y'=4,'xl'=2,'xh'=2,'c'=2] {'xh','xl'}, dimensions={0}, use_global_device_ids=true | all-gather | bytes 819200 | tf_op jit(solution)/shard_map/all_gather | solution.py:281
  70.2 1.9 %collective-permute-start = (bf16[128,2560]{1,0:T(8,128)(2,1)S(1)}, bf16[128,2560]{1,0:T(8,128)(2,1)S(1)}, u32[]{:S(2)}, u32[]{:S(2)}) collective-permute-start(bf16[128,2560]{1,0:T(8,128)(2,1)S(1)} %all_gather.3.own_ref), channel_id=1, source_target_pairs={{0,1},{1,0},{2,3},{3,2},{4,5},{5,4},{6,7},{7,6},{8,9},{9,8},{10,11... | collective-permute-start | bytes 1966088 | tf_op jit(solution)/shard_map/ppermute | solution.py:282
  72.2 2.1 %collective-permute-done.other_ref = bf16[128,2560]{1,0:T(8,128)(2,1)S(1)} collective-permute-done((bf16[128,2560]{1,0:T(8,128)(2,1)S(1)}, bf16[128,2560]{1,0:T(8,128)(2,1)S(1)}, u32[]{:S(2)}, u32[]{:S(2)}) %collective-permute-start) | collective-permute-done | bytes 655392 | tf_op jit(solution)/shard_map/ppermute | solution.py:282
  74.2 0.0 all-to-all-done.2.cols_ref
  74.2 1.9 %block_product.1 = f32[128,4,128]{2,1,0:T(4,128)} custom-call(s32[1]{0:T(128)} %bitcast.core_ref, bf16[128,2560]{1,0:T(8,128)(2,1)S(1)} %all_gather.3.own_ref, bf16[128,2560]{1,0:T(8,128)(2,1)S(1)} %collective-permute-done.other_ref, bf16[4,64,2560]{2,1,0:T(8,128)(2,1)S(1)} %all-to-all-done.2.cols_ref), custom_call_target="tpu_custom_call" | custom-call | tf_op jit(solution)/shard_map/block_product/pallas_call | solution.py:152
  76.1 11.9 %all-to-all-start.3 = ((f32[128,4,128]{2,1,0:T(4,128)}), f32[128,4,128]{2,1,0:T(4,128)S(1)}, u32[]{:S(2)}, u32[]{:S(2)}) async-start(f32[128,4,128]{2,1,0:T(4,128)} %block_product.1), calls=%async_computation.3 | async-start | bytes 524288 | tf_op jit(solution)/shard_map/all_to_all | solution.py:285
  88.0 0.1 places.1.hot_ref
  88.1 22.1 %all-to-all-done.3.parts_ref = f32[128,4,128]{2,1,0:T(4,128)S(1)} async-done(((f32[128,4,128]{2,1,0:T(4,128)}), f32[128,4,128]{2,1,0:T(4,128)S(1)}, u32[]{:S(2)}, u32[]{:S(2)}) %all-to-all-start.3) | async-done | bytes 262176 | tf_op jit(solution)/shard_map/all_to_all | solution.py:285
  110.2 0.9 finish.1
  (1 shorter events, 0.0 us)
Async XLA Ops:
  0.6 6.5 %copy-start = (bf16[8,4,5120]{2,1,0:T(4,128)(2,1)S(1)}, bf16[8,4,5120]{2,1,0:T(4,128)(2,1)}, u32[]{:S(2)}) copy-start(bf16[8,4,5120]{2,1,0:T(4,128)(2,1)} %param.4) | copy-start | bytes 983044
  2.4 9.0 %all-to-all-start = ((bf16[4,3,2,5120]{3,2,1,0:T(2,128)(2,1)}), bf16[4,3,2,5120]{3,2,1,0:T(2,128)(2,1)S(1)}, u32[]{:S(2)}, u32[]{:S(2)}) async-start(bf16[4,3,2,5120]{3,2,1,0:T(2,128)(2,1)} %pieces.1), calls=%async_computation | async-start | bytes 491520 | tf_op jit(solution)/shard_map/all_to_all | solution.py:272
  52.5 21.7 %all-to-all-start.2 = ((bf16[4,64,2560]{2,1,0:T(8,128)(2,1)}), bf16[4,64,2560]{2,1,0:T(8,128)(2,1)S(1)}, u32[]{:S(2)}, u32[]{:S(2)}) async-start(bf16[4,64,2560]{2,1,0:T(8,128)(2,1)} %spread.1), calls=%async_computation.2 | async-start | bytes 2621440 | tf_op jit(solution)/shard_map/all_to_all | solution.py:279
  70.2 4.0 %collective-permute-start = (bf16[128,2560]{1,0:T(8,128)(2,1)S(1)}, bf16[128,2560]{1,0:T(8,128)(2,1)S(1)}, u32[]{:S(2)}, u32[]{:S(2)}) collective-permute-start(bf16[128,2560]{1,0:T(8,128)(2,1)S(1)} %all_gather.3.own_ref), channel_id=1, source_target_pairs={{0,1},{1,0},{2,3},{3,2},{4,5},{5,4},{6,7},{7,6},{8,9},{9,8},{10,11... | collective-permute-start | bytes 1966088 | tf_op jit(solution)/shard_map/ppermute | solution.py:282
  76.1 34.1 %all-to-all-start.3 = ((f32[128,4,128]{2,1,0:T(4,128)}), f32[128,4,128]{2,1,0:T(4,128)S(1)}, u32[]{:S(2)}, u32[]{:S(2)}) async-start(f32[128,4,128]{2,1,0:T(4,128)} %block_product.1), calls=%async_computation.3 | async-start | bytes 524288 | tf_op jit(solution)/shard_map/all_to_all | solution.py:285

commit v8 on v6

--- a/solution.py
+++ b/solution.py
@@ -123,21 +123,32 @@
     return pltpu.roll(values, 64, 1)
 
 
-def product_kernel(core_ref, own_ref, other_ref, cols_ref, out_ref, blocks):
-    core = core_ref[0]
+def half_product(rows_ref, cols_ref):
     cols = jnp.concatenate(
         [cols_ref[y, 16 * zh : 16 * zh + 16, :] for zh in range(4) for y in range(4)], axis=0
     )
     left = lax.broadcasted_iota(jnp.int32, (64, 128), 1) < 64
-    for rows_ref, place in ((own_ref, core), (other_ref, 1 - core)):
-        block = lax.dot_general(
-            rows_ref[...], cols, (((1,), (1,)), ((), ())), preferred_element_type=jnp.float32
-        )
-        for pair in range(2):
-            low = block[:64, 128 * pair : 128 * pair + 128]
-            high = block[64:, 128 * pair : 128 * pair + 128]
-            blocks[place, 2 * pair] = jnp.where(left, low, swapped(high))
-            blocks[place, 2 * pair + 1] = jnp.where(left, swapped(low), high)
+    block = lax.dot_general(
+        rows_ref[...], cols, (((1,), (1,)), ((), ())), preferred_element_type=jnp.float32
+    )
+    pieces = []
+    for pair in range(2):
+        low = block[:64, 128 * pair : 128 * pair + 128]
+        high = block[64:, 128 * pair : 128 * pair + 128]
+        pieces += [jnp.where(left, low, swapped(high)), jnp.where(left, swapped(low), high)]
+    return pieces
+
+
+def own_kernel(own_ref, cols_ref, out_ref):
+    for zh, piece in enumerate(half_product(own_ref, cols_ref)):
+        out_ref[zh] = piece
+
+
+def join_kernel(core_ref, done_ref, other_ref, cols_ref, out_ref, blocks):
+    core = core_ref[0]
+    for zh, piece in enumerate(half_product(other_ref, cols_ref)):
+        blocks[1 - core, zh] = piece
+        blocks[core, zh] = done_ref[zh]
     for z in range(16):
         for xl in range(2):
             for zh in range(4):
@@ -147,17 +158,30 @@
                     ]
 
 
-def block_product(core, own, other, cols):
-    whole = pl.BlockSpec(memory_space=pltpu.VMEM)
-    return pl.pallas_call(
-        product_kernel,
+def own_product(own, cols):
+    whole = pl.BlockSpec(memory_space=pltpu.VMEM)
+    return pl.pallas_call(
+        own_kernel,
+        in_specs=[whole, whole],
+        out_specs=whole,
+        out_shape=jax.ShapeDtypeStruct((4, 64, 128), jnp.float32),
+        compiler_params=pltpu.CompilerParams(vmem_limit_bytes=24 * 1024 * 1024),
+        cost_estimate=pl.CostEstimate(flops=2 * 128 * 256 * SHARE, bytes_accessed=2000000, transcendentals=0),
+        name="own_product",
+    )(own, cols)
+
+
+def joined(core, done, other, cols):
+    whole = pl.BlockSpec(memory_space=pltpu.VMEM)
+    return pl.pallas_call(
+        join_kernel,
         in_specs=[pl.BlockSpec(memory_space=pltpu.SMEM), whole, whole, whole],
         out_specs=whole,
         out_shape=jax.ShapeDtypeStruct((128, 4, 128), jnp.float32),
         scratch_shapes=[pltpu.VMEM((2, 4, 64, 128), jnp.float32)],
         compiler_params=pltpu.CompilerParams(vmem_limit_bytes=24 * 1024 * 1024),
-        name="block_product",
-    )(core, own, other, cols)
+        name="joined",
+    )(core, done, other, cols)
 
 
 def finish_kernel(parts_ref, correlation_ref, projected_ref):
@@ -247,7 +271,7 @@
     rows = lax.all_gather(rows, ("xh", "xl"), axis=0, tiled=True)
     other = lax.ppermute(rows, "c", [(0, 1), (1, 0)])
     core = lax.axis_index("c").astype(jnp.int32).reshape(1)
-    partial = block_product(core, rows, other, cols)
+    partial = joined(core, own_product(rows, cols), other, cols)
     parts = lax.all_to_all(partial, ("z", "xl", "xh", "c"), split_axis=0, concat_axis=0, tiled=True)
     return tuple(finish(parts))
 

time: 111 us -> 111 us (level)
  transfers between devices with their start and end apart: 3 -> 3, of which waited for: 2 -> 2; matrix products, arithmetic and copies ran while one was open for 0% -> 0% of each run, Pallas kernels for 0% -> 1%
where the time goes in v8:
time: 111 us; the launch traced here: 110 us
  blocking collectives  82.9 us (75%)
  starting transfers between devices  11.2 us (10%)
  Pallas kernels  7.51 us (7%)
  waiting for transfers between devices  5.6 us (5%)
  local copies, waits for them, and re-layouts  1.83 us (2%)
    all_to_all x1, blocking collectives, per_device(): lax.all_to_all(shares, 'z', split_axis=0, concat_axis=0, tiled=True)  36 us
    all_to_all x1, blocking collectives, per_device(): lax.all_to_all(partial, ('z', 'xl', 'xh', 'c'), split_axis=0, concat_axis...  33.9 us
    all_gather x1, blocking collectives, per_device(): rows = lax.all_gather(rows, ('xh', 'xl'), axis=0, tiled=True)  13 us
    all_to_all x1, starting transfers between devices, per_device(): lax.all_to_all(pieces, ('xh', 'c'), split_axis=0, concat_axis=0, tiled=True)  4.81 us
    all_to_all x1, starting transfers between devices, per_device(): lax.all_to_all(jnp.broadcast_to(cols[None], (4, 4 * SHARES, SHARE)), 'y',...  4.46 us
    all_to_all x1, waiting for transfers between devices, per_device(): lax.all_to_all(pieces, ('xh', 'c'), split_axis=0, concat_axis=0, tiled=True)  4.16 us
    pallas_call x1, Pallas kernels, filtered_and_applied(): pl.pallas_call(filter_kernel, in_specs=[whole, whole], out_specs=whole, o...  3.6 us
  transfers between devices with their start and end apart: 3, of which 2 were waited for; matrix products, arithmetic and copies ran while one was open for 0% of the time, Pallas kernels for 1%

profile of v8, /device:TPU:6, one launch (start us, length us, event | category | flops | bytes accessed | tf_op | source)
XLA Modules:
  0.0 109.7 jit_solution(933902095937507678)
XLA Ops:
  0.6 0.0 copy-start
  0.6 1.7 %pieces.1 = bf16[4,3,2,5120]{3,2,1,0:T(2,128)(2,1)} custom-call(bf16[4,2,2,5120]{3,2,1,0:T(2,128)(2,1)} %bitcast.10, bf16[2,5120]{1,0:T(2,128)(2,1)} %potential_ref.1), custom_call_target="tpu_custom_call" | custom-call | tf_op jit(solution)/shard_map/pieces/pallas_call | solution.py:247
  2.4 4.8 %all-to-all-start = ((bf16[4,3,2,5120]{3,2,1,0:T(2,128)(2,1)}), bf16[4,3,2,5120]{3,2,1,0:T(2,128)(2,1)S(1)}, u32[]{:S(2)}, u32[]{:S(2)}) async-start(bf16[4,3,2,5120]{3,2,1,0:T(2,128)(2,1)} %pieces.1), calls=%async_computation | async-start | bytes 491520 | tf_op jit(solution)/shard_map/all_to_all | solution.py:261
  7.2 0.0 copy-done
  7.2 4.2 %all-to-all-done.mixed_ref = bf16[4,3,2,5120]{3,2,1,0:T(2,128)(2,1)S(1)} async-done(((bf16[4,3,2,5120]{3,2,1,0:T(2,128)(2,1)}), bf16[4,3,2,5120]{3,2,1,0:T(2,128)(2,1)S(1)}, u32[]{:S(2)}, u32[]{:S(2)}) %all-to-all-start) | async-done | bytes 245792 | tf_op jit(solution)/shard_map/all_to_all | solution.py:261
  11.4 3.6 %chebyshev_filter.1 = bf16[4,8,5120]{2,1,0:T(8,128)(2,1)S(1)} custom-call(bf16[4,3,2,5120]{3,2,1,0:T(2,128)(2,1)S(1)} %all-to-all-done.mixed_ref, bf16[2,4,5120]{2,1,0:T(4,128)(2,1)S(1)} %dynamic-slice_bitcast_fusion.rim_ref), custom_call_target="tpu_custom_call" | custom-call | tf_op jit(solution)/shard_map/chebyshev_filter/pallas_call | solution.py:106
  15.0 0.1 reshape.23
  15.1 0.3 copy.7
  15.4 36.0 %all_to_all.20 = bf16[16,4,2560]{2,1,0:T(4,128)(2,1)S(1)} all-to-all(bf16[16,4,2560]{2,1,0:T(4,128)(2,1)S(1)} %bitcast.9), channel_id=1, replica_groups=mesh['z'=16,'y'=4,'xl'=2,'xh'=2,'c'=2] {'z'}, dimensions={0} | all-to-all | bytes 655360 | tf_op jit(solution)/shard_map/all_to_all | solution.py:265
  51.3 0.1 broadcast_in_dim.7
  51.4 1.2 %broadcast_in_dim.8 = bf16[4,64,2560]{2,1,0:T(8,128)(2,1)} broadcast(bf16[64,2560]{1,0:T(8,128)(2,1)S(1)} %broadcast_in_dim.7), dimensions={1,2} | broadcast | bytes 1638400 | tf_op jit(solution)/shard_map/broadcast_in_dim | solution.py:268
  52.6 4.5 %all-to-all-start.2 = ((bf16[4,64,2560]{2,1,0:T(8,128)(2,1)}), bf16[4,64,2560]{2,1,0:T(8,128)(2,1)S(1)}, u32[]{:S(2)}, u32[]{:S(2)}) async-start(bf16[4,64,2560]{2,1,0:T(8,128)(2,1)} %broadcast_in_dim.8), calls=%async_computation.2 | async-start | bytes 2621440 | tf_op jit(solution)/shard_map/all_to_all | solution.py:267
  57.0 0.1 slice.4
  57.2 0.1 reshape.24
  57.2 13.0 %all_gather.3.own_ref = bf16[128,2560]{1,0:T(8,128)(2,1)S(1)} all-gather(bf16[32,2560]{1,0:T(8,128)(2,1)S(1)} %reshape.24), channel_id=1, replica_groups=mesh['z'=16,'y'=4,'xl'=2,'xh'=2,'c'=2] {'xh','xl'}, dimensions={0}, use_global_device_ids=true | all-gather | bytes 819200 | tf_op jit(solution)/shard_map/all_gather | solution.py:271
  70.3 1.9 %collective-permute-start = (bf16[128,2560]{1,0:T(8,128)(2,1)S(1)}, bf16[128,2560]{1,0:T(8,128)(2,1)S(1)}, u32[]{:S(2)}, u32[]{:S(2)}) collective-permute-start(bf16[128,2560]{1,0:T(8,128)(2,1)S(1)} %all_gather.3.own_ref), channel_id=1, source_target_pairs={{0,1},{1,0},{2,3},{3,2},{4,5},{5,4},{6,7},{7,6},{8,9},{9,8},{10,11... | collective-permute-start | bytes 1966088 | tf_op jit(solution)/shard_map/ppermute | solution.py:272
  72.2 0.0 all-to-all-done.2.cols_ref
  72.2 0.6 own_product.1.done_ref
  72.8 1.4 %collective-permute-done.other_ref = bf16[128,2560]{1,0:T(8,128)(2,1)S(1)} collective-permute-done((bf16[128,2560]{1,0:T(8,128)(2,1)S(1)}, bf16[128,2560]{1,0:T(8,128)(2,1)S(1)}, u32[]{:S(2)}, u32[]{:S(2)}) %collective-permute-start) | collective-permute-done | bytes 655392 | tf_op jit(solution)/shard_map/ppermute | solution.py:272
  74.3 0.7 joined.1
  75.0 33.9 %all_to_all.21.parts_ref = f32[128,4,128]{2,1,0:T(4,128)S(1)} all-to-all(f32[128,4,128]{2,1,0:T(4,128)S(1)} %joined.1), channel_id=1, replica_groups=mesh['z'=16,'y'=4,'xl'=2,'xh'=2,'c'=2] {'z','xl','xh','c'}, dimensions={0} | all-to-all | bytes 524288 | tf_op jit(solution)/shard_map/all_to_all | solution.py:275
  108.9 0.9 finish.1
  (1 shorter events, 0.0 us)
Async XLA Ops:
  0.6 6.5 %copy-start = (bf16[8,4,5120]{2,1,0:T(4,128)(2,1)S(1)}, bf16[8,4,5120]{2,1,0:T(4,128)(2,1)}, u32[]{:S(2)}) copy-start(bf16[8,4,5120]{2,1,0:T(4,128)(2,1)} %param.4) | copy-start | bytes 983044
  2.4 9.0 %all-to-all-start = ((bf16[4,3,2,5120]{3,2,1,0:T(2,128)(2,1)}), bf16[4,3,2,5120]{3,2,1,0:T(2,128)(2,1)S(1)}, u32[]{:S(2)}, u32[]{:S(2)}) async-start(bf16[4,3,2,5120]{3,2,1,0:T(2,128)(2,1)} %pieces.1), calls=%async_computation | async-start | bytes 491520 | tf_op jit(solution)/shard_map/all_to_all | solution.py:261
  52.6 19.6 %all-to-all-start.2 = ((bf16[4,64,2560]{2,1,0:T(8,128)(2,1)}), bf16[4,64,2560]{2,1,0:T(8,128)(2,1)S(1)}, u32[]{:S(2)}, u32[]{:S(2)}) async-start(bf16[4,64,2560]{2,1,0:T(8,128)(2,1)} %broadcast_in_dim.8), calls=%async_computation.2 | async-start | bytes 2621440 | tf_op jit(solution)/shard_map/all_to_all | solution.py:267
  70.3 4.0 %collective-permute-start = (bf16[128,2560]{1,0:T(8,128)(2,1)S(1)}, bf16[128,2560]{1,0:T(8,128)(2,1)S(1)}, u32[]{:S(2)}, u32[]{:S(2)}) collective-permute-start(bf16[128,2560]{1,0:T(8,128)(2,1)S(1)} %all_gather.3.own_ref), channel_id=1, source_target_pairs={{0,1},{1,0},{2,3},{3,2},{4,5},{5,4},{6,7},{7,6},{8,9},{9,8},{10,11... | collective-permute-start | bytes 1966088 | tf_op jit(solution)/shard_map/ppermute | solution.py:272

commit v9 on v8

--- a/solution.py
+++ b/solution.py
@@ -188,10 +188,10 @@
     left = lax.broadcasted_iota(jnp.int32, (4, 128), 1) < 64
     pieces = []
     for pair in range(4):
-        one, two = parts_ref[2 * pair], parts_ref[2 * pair + 1]
+        both = parts_ref[pair]
         for k in range(1, 16):
-            one = one + parts_ref[8 * k + 2 * pair]
-            two = two + parts_ref[8 * k + 2 * pair + 1]
+            both = both + parts_ref[4 * k + pair]
+        one, two = both[:4], both[4:]
         low = jnp.where(left, one, swapped(two))
         high = jnp.where(left, swapped(one), two)
         pieces.append(jnp.concatenate([low, high], axis=0))
@@ -273,7 +273,7 @@
     core = lax.axis_index("c").astype(jnp.int32).reshape(1)
     partial = joined(core, own_product(rows, cols), other, cols)
     parts = lax.all_to_all(partial, ("z", "xl", "xh", "c"), split_axis=0, concat_axis=0, tiled=True)
-    return tuple(finish(parts))
+    return tuple(finish(parts.reshape(64, 8, 128)))
 
 
 def solution(mesh):

time: 111 us -> 111 us (level)
  no operation moved by 1% of the time
where the time goes in v9:
time: 111 us; the launch traced here: 110 us
  blocking collectives  82.9 us (75%)
  starting transfers between devices  11.2 us (10%)
  Pallas kernels  7.5 us (7%)
  waiting for transfers between devices  5.6 us (5%)
  local copies, waits for them, and re-layouts  1.83 us (2%)
    all_to_all x1, blocking collectives, per_device(): lax.all_to_all(shares, 'z', split_axis=0, concat_axis=0, tiled=True)  36 us
    all_to_all x1, blocking collectives, per_device(): lax.all_to_all(partial, ('z', 'xl', 'xh', 'c'), split_axis=0, concat_axis...  33.9 us
    all_gather x1, blocking collectives, per_device(): rows = lax.all_gather(rows, ('xh', 'xl'), axis=0, tiled=True)  13 us
    all_to_all x1, starting transfers between devices, per_device(): lax.all_to_all(pieces, ('xh', 'c'), split_axis=0, concat_axis=0, tiled=True)  4.81 us
    all_to_all x1, starting transfers between devices, per_device(): lax.all_to_all(jnp.broadcast_to(cols[None], (4, 4 * SHARES, SHARE)), 'y',...  4.46 us
    all_to_all x1, waiting for transfers between devices, per_device(): lax.all_to_all(pieces, ('xh', 'c'), split_axis=0, concat_axis=0, tiled=True)  4.16 us
    pallas_call x1, Pallas kernels, filtered_and_applied(): pl.pallas_call(filter_kernel, in_specs=[whole, whole], out_specs=whole, o...  3.6 us
  transfers between devices with their start and end apart: 3, of which 2 were waited for; matrix products, arithmetic and copies ran while one was open for 0% of the time, Pallas kernels for 1%

profile of v9, /device:TPU:6, one launch (start us, length us, event | category | flops | bytes accessed | tf_op | source)
XLA Modules:
  0.0 109.7 jit_solution(9681177517875842185)
XLA Ops:
  0.6 0.0 copy-start
  0.6 1.7 %pieces.1 = bf16[4,3,2,5120]{3,2,1,0:T(2,128)(2,1)} custom-call(bf16[4,2,2,5120]{3,2,1,0:T(2,128)(2,1)} %bitcast.12, bf16[2,5120]{1,0:T(2,128)(2,1)} %potential_ref.1), custom_call_target="tpu_custom_call" | custom-call | tf_op jit(solution)/shard_map/pieces/pallas_call | solution.py:247
  2.4 4.8 %all-to-all-start = ((bf16[4,3,2,5120]{3,2,1,0:T(2,128)(2,1)}), bf16[4,3,2,5120]{3,2,1,0:T(2,128)(2,1)S(1)}, u32[]{:S(2)}, u32[]{:S(2)}) async-start(bf16[4,3,2,5120]{3,2,1,0:T(2,128)(2,1)} %pieces.1), calls=%async_computation | async-start | bytes 491520 | tf_op jit(solution)/shard_map/all_to_all | solution.py:261
  7.2 0.0 copy-done
  7.2 4.2 %all-to-all-done.mixed_ref = bf16[4,3,2,5120]{3,2,1,0:T(2,128)(2,1)S(1)} async-done(((bf16[4,3,2,5120]{3,2,1,0:T(2,128)(2,1)}), bf16[4,3,2,5120]{3,2,1,0:T(2,128)(2,1)S(1)}, u32[]{:S(2)}, u32[]{:S(2)}) %all-to-all-start) | async-done | bytes 245792 | tf_op jit(solution)/shard_map/all_to_all | solution.py:261
  11.4 3.6 %chebyshev_filter.1 = bf16[4,8,5120]{2,1,0:T(8,128)(2,1)S(1)} custom-call(bf16[4,3,2,5120]{3,2,1,0:T(2,128)(2,1)S(1)} %all-to-all-done.mixed_ref, bf16[2,4,5120]{2,1,0:T(4,128)(2,1)S(1)} %dynamic-slice_bitcast_fusion.rim_ref), custom_call_target="tpu_custom_call" | custom-call | tf_op jit(solution)/shard_map/chebyshev_filter/pallas_call | solution.py:106
  15.0 0.1 reshape.26
  15.1 0.3 copy.7
  15.4 36.0 %all_to_all.20 = bf16[16,4,2560]{2,1,0:T(4,128)(2,1)S(1)} all-to-all(bf16[16,4,2560]{2,1,0:T(4,128)(2,1)S(1)} %bitcast.11), channel_id=1, replica_groups=mesh['z'=16,'y'=4,'xl'=2,'xh'=2,'c'=2] {'z'}, dimensions={0} | all-to-all | bytes 655360 | tf_op jit(solution)/shard_map/all_to_all | solution.py:265
  51.3 0.1 broadcast_in_dim.7
  51.4 1.2 %broadcast_in_dim.8 = bf16[4,64,2560]{2,1,0:T(8,128)(2,1)} broadcast(bf16[64,2560]{1,0:T(8,128)(2,1)S(1)} %broadcast_in_dim.7), dimensions={1,2} | broadcast | bytes 1638400 | tf_op jit(solution)/shard_map/broadcast_in_dim | solution.py:268
  52.6 4.5 %all-to-all-start.2 = ((bf16[4,64,2560]{2,1,0:T(8,128)(2,1)}), bf16[4,64,2560]{2,1,0:T(8,128)(2,1)S(1)}, u32[]{:S(2)}, u32[]{:S(2)}) async-start(bf16[4,64,2560]{2,1,0:T(8,128)(2,1)} %broadcast_in_dim.8), calls=%async_computation.2 | async-start | bytes 2621440 | tf_op jit(solution)/shard_map/all_to_all | solution.py:267
  57.0 0.1 slice.4
  57.2 0.1 reshape.27
  57.2 13.0 %all_gather.3.own_ref = bf16[128,2560]{1,0:T(8,128)(2,1)S(1)} all-gather(bf16[32,2560]{1,0:T(8,128)(2,1)S(1)} %reshape.27), channel_id=1, replica_groups=mesh['z'=16,'y'=4,'xl'=2,'xh'=2,'c'=2] {'xh','xl'}, dimensions={0}, use_global_device_ids=true | all-gather | bytes 819200 | tf_op jit(solution)/shard_map/all_gather | solution.py:271
  70.3 1.9 %collective-permute-start = (bf16[128,2560]{1,0:T(8,128)(2,1)S(1)}, bf16[128,2560]{1,0:T(8,128)(2,1)S(1)}, u32[]{:S(2)}, u32[]{:S(2)}) collective-permute-start(bf16[128,2560]{1,0:T(8,128)(2,1)S(1)} %all_gather.3.own_ref), channel_id=1, source_target_pairs={{0,1},{1,0},{2,3},{3,2},{4,5},{5,4},{6,7},{7,6},{8,9},{9,8},{10,11... | collective-permute-start | bytes 1966088 | tf_op jit(solution)/shard_map/ppermute | solution.py:272
  72.2 0.0 all-to-all-done.2.cols_ref
  72.2 0.6 own_product.1.done_ref
  72.8 1.4 %collective-permute-done.other_ref = bf16[128,2560]{1,0:T(8,128)(2,1)S(1)} collective-permute-done((bf16[128,2560]{1,0:T(8,128)(2,1)S(1)}, bf16[128,2560]{1,0:T(8,128)(2,1)S(1)}, u32[]{:S(2)}, u32[]{:S(2)}) %collective-permute-start) | collective-permute-done | bytes 655392 | tf_op jit(solution)/shard_map/ppermute | solution.py:272
  74.3 0.7 joined.1
  75.0 33.9 %all_to_all.21 = f32[128,4,128]{2,1,0:T(4,128)S(1)} all-to-all(f32[128,4,128]{2,1,0:T(4,128)S(1)} %joined.1), channel_id=1, replica_groups=mesh['z'=16,'y'=4,'xl'=2,'xh'=2,'c'=2] {'z','xl','xh','c'}, dimensions={0} | all-to-all | bytes 524288 | tf_op jit(solution)/shard_map/all_to_all | solution.py:275
  108.9 0.9 finish.1
  (1 shorter events, 0.0 us)
Async XLA Ops:
  0.6 6.5 %copy-start = (bf16[8,4,5120]{2,1,0:T(4,128)(2,1)S(1)}, bf16[8,4,5120]{2,1,0:T(4,128)(2,1)}, u32[]{:S(2)}) copy-start(bf16[8,4,5120]{2,1,0:T(4,128)(2,1)} %param.4) | copy-start | bytes 983044
  2.4 9.0 %all-to-all-start = ((bf16[4,3,2,5120]{3,2,1,0:T(2,128)(2,1)}), bf16[4,3,2,5120]{3,2,1,0:T(2,128)(2,1)S(1)}, u32[]{:S(2)}, u32[]{:S(2)}) async-start(bf16[4,3,2,5120]{3,2,1,0:T(2,128)(2,1)} %pieces.1), calls=%async_computation | async-start | bytes 491520 | tf_op jit(solution)/shard_map/all_to_all | solution.py:261
  52.6 19.6 %all-to-all-start.2 = ((bf16[4,64,2560]{2,1,0:T(8,128)(2,1)}), bf16[4,64,2560]{2,1,0:T(8,128)(2,1)S(1)}, u32[]{:S(2)}, u32[]{:S(2)}) async-start(bf16[4,64,2560]{2,1,0:T(8,128)(2,1)} %broadcast_in_dim.8), calls=%async_computation.2 | async-start | bytes 2621440 | tf_op jit(solution)/shard_map/all_to_all | solution.py:267
  70.3 4.0 %collective-permute-start = (bf16[128,2560]{1,0:T(8,128)(2,1)S(1)}, bf16[128,2560]{1,0:T(8,128)(2,1)S(1)}, u32[]{:S(2)}, u32[]{:S(2)}) collective-permute-start(bf16[128,2560]{1,0:T(8,128)(2,1)S(1)} %all_gather.3.own_ref), channel_id=1, source_target_pairs={{0,1},{1,0},{2,3},{3,2},{4,5},{5,4},{6,7},{7,6},{8,9},{9,8},{10,11... | collective-permute-start | bytes 1966088 | tf_op jit(solution)/shard_map/ppermute | solution.py:272
